TPU v7x, 32 devices: a whole 2x2x4 slice. The times are simulated.
32 devices in a mesh: groups: 2 (over y), ctx: 16 (over z, x, core).
Axes of the slice: x: 2, y: 2, z: 4, core: 2. Of those that a mesh axis runs over, the one named last changes fastest.
Arguments:
- query_vectors: bfloat16 [16384, 2048], P(('groups', 'ctx')), parts along dimension 0, may hold values from -60 to 60
- key_vectors: bfloat16 [16384, 2048], P(('groups', 'ctx')), parts along dimension 0, may hold values from -6 to 6
- value_vectors: bfloat16 [16384, 2048], P(('groups', 'ctx')), parts along dimension 0, may hold values from -8 to 8
- out_weight: bfloat16 [2048, 2048], P(None, 'ctx'), may hold values from -0.125 to 0.125
Outputs:
- projected: bfloat16 [16384, 2048], P(('groups', 'ctx')), parts along dimension 0
There are 2 independent parts, one for each index of `groups`. A program takes and returns all parts, laid end to end along the dimension named above; an argument that names none is the same for every part. Nothing has to cross between parts.
All inputs are finite; a program needn't handle non-finite values.
Results may differ from a plain program's by a relative error of at most 0.0095.
Values may be sent and summed in bfloat16 or wider, within the bound.
No kernel may reach another device: no remote copies, remote signals or barrier semaphores. Data moves between devices by JAX's collectives and lax.ppermute only.
A program may use at most 192 MiB of HBM per device.

v0:
```python
import jax
import jax.numpy as jnp
from jax import lax
from jax.sharding import PartitionSpec as P

HEADS = 16
HEAD_DIM = 128
BLOCK = 128
LEVELS = 5


def shifted(block, axis, distance):
    devices = range(lax.axis_size(axis))
    route = [(i - distance, i) for i in devices if i - distance in devices]
    return lax.ppermute(block, axis, route)


def padded(block, sides, width):
    for axis, dim in sides:
        count = lax.axis_size(axis)
        forward = [(i, i + 1) for i in range(count - 1)]
        backward = [(target, source) for source, target in forward]
        low = lax.ppermute(
            lax.slice_in_dim(block, block.shape[dim] - width, None, axis=dim), axis, forward
        )
        high = lax.ppermute(lax.slice_in_dim(block, 0, width, axis=dim), axis, backward)
        block = jnp.concatenate([low, block, high], axis=dim)
    return block


def coarsen(matrix):
    paired = matrix.reshape(matrix.shape[0] // 2, 2, matrix.shape[1]).astype(jnp.float32)
    return ((paired[:, 0] + paired[:, 1]) * 0.5).astype(jnp.bfloat16)


def key_valid(height, block_index, row_pos, nblocks):
    grid_shape = (block_index.shape[0], row_pos.shape[0], BLOCK)
    has_left = jnp.broadcast_to((block_index >= 1)[:, None, None], grid_shape)
    has_right = jnp.broadcast_to((block_index + 1 < nblocks)[:, None, None], grid_shape)
    if height == 0:
        return jnp.concatenate([has_left, jnp.ones(grid_shape, jnp.bool_), has_right], axis=2)
    upper_half = (row_pos >= BLOCK // 2)[None, :, None]
    key_place = jnp.arange(BLOCK, dtype=jnp.int32)[None, None, :]
    left_ok = has_left & (upper_half | (key_place < BLOCK // 2))
    right_ok = has_right & (jnp.logical_not(upper_half) | (key_place >= BLOCK // 2))
    return jnp.concatenate([left_ok, right_ok], axis=2)


def attend(queries, keys_window, values_window, admitted):
    score_scale = HEAD_DIM ** (-0.5)
    mask_bias = jnp.where(admitted, 0.0, -jnp.inf).astype(jnp.float32)[:, None, :, :]
    scores = (
        jnp.einsum("nrhd,nkhd->nhrk", queries, keys_window, preferred_element_type=jnp.float32)
        * score_scale
        + mask_bias
    )
    row_peak = jnp.max(scores, axis=3)
    weights = jnp.exp(scores - row_peak[:, :, :, None]).astype(jnp.bfloat16)
    numerator = jnp.einsum(
        "nhrk,nkhd->nrhd", weights, values_window, preferred_element_type=jnp.float32
    )
    denominator = jnp.sum(weights.astype(jnp.float32), axis=3)
    return (jnp.transpose(row_peak, (0, 2, 1)), numerator, jnp.transpose(denominator, (0, 2, 1)))


def neighbour_blocks(key_value, span_devs, position):
    coarse_rows = key_value.shape[1]
    pieces = []
    for offset in range(1 - 2 * span_devs, 2 * span_devs):
        if offset == 0:
            pieces.append(key_value)
        else:
            pieces.append(shifted(key_value, "ctx", -offset))
    window = jnp.concatenate(pieces, axis=1)
    slice_start = (span_devs - 1 - position % span_devs) * coarse_rows
    left_keys = lax.dynamic_slice_in_dim(window, slice_start, BLOCK, 1)
    right_keys = lax.dynamic_slice_in_dim(window, slice_start + 2 * BLOCK, BLOCK, 1)
    return (left_keys, right_keys)


def merge_levels(peaks, numerators, denominators):
    spread = [jnp.repeat(peaks[height], 1 << height, axis=0) for height in range(len(peaks))]
    highest = spread[0]
    for level_peak in spread[1:]:
        highest = jnp.maximum(highest, level_peak)
    weighted = 0.0
    normaliser = 0.0
    for height in range(len(peaks)):
        factor = float(1 << height) * jnp.exp(spread[height] - highest)
        weighted = weighted + factor[:, :, None] * jnp.repeat(
            numerators[height], 1 << height, axis=0
        )
        normaliser = normaliser + factor * jnp.repeat(denominators[height], 1 << height, axis=0)
    return weighted / normaliser[:, :, None]


def per_device(query_vectors, key_vectors, value_vectors, out_weight):
    ctx_size = lax.axis_size("ctx")
    position = lax.axis_index("ctx")
    local_rows = query_vectors.shape[0]
    channels = query_vectors.shape[1]
    query_levels = [query_vectors]
    pair_levels = [jnp.stack([key_vectors, value_vectors])]
    for height in range(1, LEVELS):
        query_levels.append(coarsen(query_levels[-1]))
        previous = pair_levels[-1]
        pair_levels.append(jnp.stack([coarsen(previous[0]), coarsen(previous[1])]))
    local_levels = [height for height in range(LEVELS) if local_rows >> height >= BLOCK]
    rim_pairs = {}
    for height in local_levels:
        grown = padded(pair_levels[height], (("ctx", 1),), BLOCK)
        rim_pairs[height] = (grown[:, :BLOCK], grown[:, -BLOCK:])
    peaks, numerators, denominators = ([], [], [])
    for height in range(LEVELS):
        coarse_rows = local_rows >> height
        nblocks = local_rows * ctx_size // (BLOCK << height)
        key_value = pair_levels[height]
        if coarse_rows >= BLOCK:
            query_blocks = coarse_rows // BLOCK
            row_count = BLOCK
            left_rim, right_rim = rim_pairs[height]
            left_keys = jnp.concatenate([left_rim, key_value[:, : coarse_rows - BLOCK]], axis=1)
            right_keys = jnp.concatenate([key_value[:, BLOCK:], right_rim], axis=1)
            block_index = position * query_blocks + jnp.arange(query_blocks, dtype=jnp.int32)
            row_pos = jnp.arange(BLOCK, dtype=jnp.int32)
        else:
            span_devs = BLOCK // coarse_rows
            query_blocks = 1
            row_count = coarse_rows
            left_keys, right_keys = neighbour_blocks(key_value, span_devs, position)
            block_index = (position // span_devs)[None]
            row_pos = position % span_devs * coarse_rows + jnp.arange(coarse_rows, dtype=jnp.int32)
        grouped = (2, query_blocks, BLOCK, HEADS, HEAD_DIM)
        parts_list = [left_keys.reshape(grouped)]
        if height == 0:
            parts_list.append(key_value.reshape(grouped))
        parts_list.append(right_keys.reshape(grouped))
        window = jnp.concatenate(parts_list, axis=2)
        queries = query_levels[height].reshape(query_blocks, row_count, HEADS, HEAD_DIM)
        admitted = key_valid(height, block_index, row_pos, nblocks)
        row_peak, numerator, denominator = attend(queries, window[0], window[1], admitted)
        peaks.append(row_peak.reshape(coarse_rows, HEADS))
        numerators.append(numerator.reshape(coarse_rows, HEADS, HEAD_DIM))
        denominators.append(denominator.reshape(coarse_rows, HEADS))
    attended = (
        merge_levels(peaks, numerators, denominators)
        .astype(jnp.bfloat16)
        .reshape(local_rows, channels)
    )
    projected = jnp.dot(
        attended,
        lax.all_gather(out_weight, "ctx", axis=1, tiled=True),
        preferred_element_type=jnp.float32,
    )
    return projected.astype(jnp.bfloat16)


def solution(mesh):
    in_specs = (
        P(("groups", "ctx"), None),
        P(("groups", "ctx"), None),
        P(("groups", "ctx"), None),
        P(None, "ctx"),
    )
    out_specs = P(("groups", "ctx"), None)
    return jax.shard_map(
        per_device, mesh=mesh, in_specs=in_specs, out_specs=out_specs, check_vma=False
    )
```

profile of v0, /device:TPU:10, one launch (start us, length us, event | category | flops | bytes accessed | tf_op | source)
XLA Modules:
  0.0 534.5 jit_solution(1131327903527137976)
XLA Ops:
  6.5 5.4 %reshape.1190 = f32[256,2,2048]{2,1,0:T(2,128)} reshape(bf16[512,2048]{1,0:T(8,128)(2,1)} %param.5) | data formatting | bytes 6291456 | tf_op jit(solution)/shard_map/convert_element_type | solution.py:32
  12.0 13.1 %convert_reduce_fusion.3 = (f32[256,2048]{1,0:T(8,128)}, bf16[256,1,2048]{2,1,0:T(2,128)(2,1)}) fusion(f32[256,2,2048]{2,1,0:T(2,128)} %reshape.1190), kind=kLoop, calls=%fused_computation.60 | loop fusion | flops 2097152 | bytes 7340032 | tf_op jit(solution)/shard_map/convert_element_type | solution.py:32
  48.3 13.3 %convert_reduce_fusion.2 = (f32[256,2048]{1,0:T(8,128)}, bf16[256,1,2048]{2,1,0:T(2,128)(2,1)}) fusion(f32[256,2,2048]{2,1,0:T(2,128)} %reshape.1191), kind=kLoop, calls=%fused_computation.59 | loop fusion | flops 2097152 | bytes 7340032 | tf_op jit(solution)/shard_map/convert_element_type | solution.py:32
  65.0 5.7 %fusion.92 = (f32[128,1,2048]{2,1,0:T(1,128)}, f32[128,1,2048]{2,1,0:T(1,128)}) fusion(f32[128,2,2048]{2,1,0:T(2,128)} %reshape.1194), kind=kLoop, calls=%fused_computation.218 | loop fusion | bytes 4194304 | tf_op jit(solution)/shard_map/slice | solution.py:33
  99.7 6.5 %collective-permute-start.13 = (bf16[2,32,2048]{2,1,0:T(8,128)(2,1)}, bf16[2,32,2048]{2,1,0:T(8,128)(2,1)}, u32[]{:S(2)}, u32[]{:S(2)}) collective-permute-start(bf16[2,32,2048]{2,1,0:T(8,128)(2,1)} %pad_maximum_fusion.12), channel_id=1, source_target_pairs={{0,6},{1,7},{2,8},{3,9},{4,10},{5,11},{6,12},{7,13},{8,14},{9,15},... | collective-permute-start | bytes 786440 | tf_op jit(solution)/shard_map/ppermute | solution.py:15
  115.0 5.5 %reshape.1189 = f32[256,2,2048]{2,1,0:T(2,128)} reshape(bf16[512,2048]{1,0:T(8,128)(2,1)} %param.4) | data formatting | bytes 6291456 | tf_op jit(solution)/shard_map/convert_element_type | solution.py:32
  120.5 12.3 %convert_reduce_fusion.6 = (bf16[256,2048]{1,0:T(8,128)(2,1)}, bf16[256,1,2048]{2,1,0:T(2,128)(2,1)S(1)}) fusion(f32[256,2,2048]{2,1,0:T(2,128)} %reshape.1189), kind=kLoop, calls=%fused_computation.65 | loop fusion | flops 1572864 | bytes 6291456 | tf_op jit(solution)/shard_map/convert_element_type | solution.py:33
  132.8 7.3 %convert_reduce_fusion.4 = f32[256,2048]{1,0:T(8,128)} fusion(bf16[256,1,2048]{2,1,0:T(2,128)(2,1)S(1)} %get-tuple-element.12), kind=kLoop, calls=%fused_computation.61 | loop fusion | flops 524288 | bytes 3145728 | tf_op jit(solution)/shard_map/convert_element_type | solution.py:32
  143.5 5.7 %fusion.90 = (f32[128,1,2048]{2,1,0:T(1,128)}, f32[128,1,2048]{2,1,0:T(1,128)}) fusion(f32[128,2,2048]{2,1,0:T(2,128)} %reshape.1192), kind=kLoop, calls=%fused_computation.216 | loop fusion | bytes 4194304 | tf_op jit(solution)/shard_map/slice | solution.py:33
  200.6 6.9 %collective-permute-done.14 = bf16[2,32,2048]{2,1,0:T(8,128)(2,1)S(1)} collective-permute-done((bf16[2,32,2048]{2,1,0:T(8,128)(2,1)}, bf16[2,32,2048]{2,1,0:T(8,128)(2,1)S(1)}, u32[]{:S(2)}, u32[]{:S(2)}) %collective-permute-start.14) | collective-permute-done | bytes 262176 | tf_op jit(solution)/shard_map/ppermute | solution.py:15
  229.7 6.5 %collective-permute-done.19 = bf16[2,32,2048]{2,1,0:T(8,128)(2,1)S(1)} collective-permute-done((bf16[2,32,2048]{2,1,0:T(8,128)(2,1)}, bf16[2,32,2048]{2,1,0:T(8,128)(2,1)S(1)}, u32[]{:S(2)}, u32[]{:S(2)}) %collective-permute-start.19) | collective-permute-done | bytes 262176 | tf_op jit(solution)/shard_map/ppermute | solution.py:15
  241.6 5.3 collective-permute-done.21
  250.9 5.4 %collective-permute-start.10 = (bf16[2,64,2048]{2,1,0:T(8,128)(2,1)}, bf16[2,64,2048]{2,1,0:T(8,128)(2,1)}, u32[]{:S(2)}, u32[]{:S(2)}) collective-permute-start(bf16[2,64,2048]{2,1,0:T(8,128)(2,1)} %pad_maximum_fusion.11), channel_id=1, source_target_pairs={{2,0},{3,1},{4,2},{5,3},{6,4},{7,5},{8,6},{9,7},{10,8},{11,9},{12,... | collective-permute-start | bytes 1572872 | tf_op jit(solution)/shard_map/ppermute | solution.py:15
  279.8 9.4 %collective-permute-done.6 = bf16[2,64,2048]{2,1,0:T(8,128)(2,1)} collective-permute-done((bf16[2,64,2048]{2,1,0:T(8,128)(2,1)}, bf16[2,64,2048]{2,1,0:T(8,128)(2,1)}, u32[]{:S(2)}, u32[]{:S(2)}) %collective-permute-start.6) | collective-permute-done | bytes 524320 | tf_op jit(solution)/shard_map/ppermute | solution.py:15
  292.2 8.9 %collective-permute-start.5 = (bf16[2,128,2048]{1,2,0:T(8,128)(2,1)}, bf16[2,128,2048]{1,2,0:T(8,128)(2,1)}, u32[]{:S(2)}, u32[]{:S(2)}) collective-permute-start(bf16[2,128,2048]{1,2,0:T(8,128)(2,1)} %pad_maximum_fusion.10), channel_id=1, source_target_pairs={{1,0},{2,1},{3,2},{4,3},{5,4},{6,5},{7,6},{8,7},{9,8},{10,9},{11,1... | collective-permute-start | bytes 3145736 | tf_op jit(solution)/shard_map/ppermute | solution.py:26
  305.5 4.5 collective-permute-start
  329.9 17.6 %collective-permute-done.5 = bf16[2,128,2048]{1,2,0:T(8,128)(2,1)} collective-permute-done((bf16[2,128,2048]{1,2,0:T(8,128)(2,1)}, bf16[2,128,2048]{1,2,0:T(8,128)(2,1)}, u32[]{:S(2)}, u32[]{:S(2)}) %collective-permute-start.5) | collective-permute-done | bytes 1048608 | tf_op jit(solution)/shard_map/ppermute | solution.py:26
  355.9 19.8 %collective-permute-done.2 = bf16[2,128,2048]{2,1,0:T(8,128)(2,1)} collective-permute-done((bf16[2,128,2048]{2,1,0:T(8,128)(2,1)}, bf16[2,128,2048]{2,1,0:T(8,128)(2,1)}, u32[]{:S(2)}, u32[]{:S(2)}) %collective-permute-start.2) | collective-permute-done | bytes 1048608 | tf_op jit(solution)/shard_map/ppermute | solution.py:23
  411.2 9.3 %pad_maximum_fusion = bf16[2,4,384,16,128]{4,2,3,1,0:T(8,128)(2,1)S(1)} fusion(bf16[2,4,128,16,128]{4,2,3,1,0:T(8,128)(2,1)S(1)} %copy.295, bf16[1,4,128,16,128]{4,2,3,1,0:T(8,128)(2,1)} %copy.293, bf16[1,4,128,16,128]{4,2,3,1,0:T(8,128)(2,1)} %copy.292, bf16[2,4,128,16,128]{4,2,3,1,0:T(8,128)(2,1)S(1)} %copy.294), kind=kLoop, calls=%fused_computation | loop fusion | flops 50331648 | bytes 25165824 | tf_op jit(solution)/shard_map/concatenate | solution.py:138
  420.6 6.0 %fusion = (f32[4,16,128]{2,1,0:T(8,128)S(1)}, f32[4,16,384,128]{3,2,1,0:T(8,128)}) fusion(f32[4,128,384]{1,2,0:T(8,128)S(1)} %add_select_fusion, bf16[4,128,16,128]{3,2,1,0:T(8,128)(2,1)S(1)} %bitcast.302, bf16[2,4,384,16,128]{4,2,3,1,0:T(8,128)(2,1)S(1)} %pad_maximum_fusion), kind=kOutput, calls=%fused_computation.4 | convolution fusion | flops 814735360 | bytes 21790720 | tf_op jit(solution)/shard_map/nrhd,nkhd->nhrk/dot_general | solution.py:53
  428.9 12.4 %fusion.11 = f32[4,128,16,128]{1,3,2,0:T(8,128)} fusion(bf16[2,4,384,16,128]{4,2,3,1,0:T(8,128)(2,1)} %copy-done, f32[4,16,384,128]{3,2,1,0:T(8,128)} %get-tuple-element.52, f32[4,16,128]{2,1,0:T(8,128)S(1)} %get-tuple-element.51, f32[4,128,384]{1,2,0:T(8,128)S(1)} %add_select_fusion), kind=kOutput, calls=%fused_computation.35 | convolution fusion | flops 817889280 | bytes 23887872 | tf_op jit(solution)/shard_map/nhrk,nkhd->nrhd/dot_general | solution.py:59
  441.3 5.4 %copy.341 = f32[4,128,16,128]{3,2,1,0:T(8,128)} copy(f32[4,128,16,128]{1,3,2,0:T(8,128)} %fusion.11) | data formatting | bytes 8388608 | tf_op jit(solution)/shard_map/nhrk,nkhd->nrhd/transpose | solution.py:59
  446.7 7.7 %convert_reduce_fusion = f32[4,16,128]{2,1,0:T(8,128)S(1)} fusion(f32[4,16,128]{2,1,0:T(8,128)S(1)} %get-tuple-element.51, f32[4,128,384]{1,2,0:T(8,128)S(1)} %add_select_fusion, f32[4,16,384,128]{3,2,1,0:T(8,128)} %get-tuple-element.52), kind=kLoop, calls=%fused_computation.2 | loop fusion | flops 18866176 | bytes 13434880 | tf_op jit(solution)/shard_map/reduce_sum | solution.py:62
  480.0 47.2 %convolution_convert_fusion = bf16[512,2048]{1,0:T(8,128)(2,1)} fusion(bf16[2048,2048]{1,0:T(8,128)(2,1)} %all-gather.2.cloned.1.call-done, f32[64,8,16,128]{3,2,1,0:T(8,128)} %bitcast.324, f32[64,8,16,128]{3,2,1,0:T(8,128)} %bitcast.318, f32[64,8,16,128]{3,2,1,0:T(8,128)} %bitcast.320, f32[64,8,16,128]{3,2,1,0:T(8,128)} %bitcast.321, ...), kind=kOutput, calls=%fused_computation.34 | convolution fusion | flops 4307550208 | bytes 52953088 | tf_op jit(solution)/shard_map/dot_general | solution.py:150
  (286 shorter events, 272.3 us)
Async XLA Ops:
  6.5 449.5 %all-gather.2.cloned.1.call-start = ((), (), s32[]{:S(2)}) async-start(), calls=%async_computation | async-start | bytes 8912896 | tf_op jit(solution)/shard_map/all_gather | solution.py:152
  94.6 168.7 %collective-permute-start.25 = (bf16[2,32,2048]{2,1,0:T(8,128)(2,1)}, bf16[2,32,2048]{2,1,0:T(8,128)(2,1)}, u32[]{:S(2)}, u32[]{:S(2)}) collective-permute-start(bf16[2,32,2048]{2,1,0:T(8,128)(2,1)} %pad_maximum_fusion.12), channel_id=1, source_target_pairs={{7,0},{8,1},{9,2},{10,3},{11,4},{12,5},{13,6},{14,7},{15,8},{23,16... | collective-permute-start | bytes 786440 | tf_op jit(solution)/shard_map/ppermute | solution.py:15
  95.8 163.9 %collective-permute-start.24 = (bf16[2,32,2048]{2,1,0:T(8,128)(2,1)}, bf16[2,32,2048]{2,1,0:T(8,128)(2,1)}, u32[]{:S(2)}, u32[]{:S(2)}) collective-permute-start(bf16[2,32,2048]{2,1,0:T(8,128)(2,1)} %pad_maximum_fusion.12), channel_id=1, source_target_pairs={{6,0},{7,1},{8,2},{9,3},{10,4},{11,5},{12,6},{13,7},{14,8},{15,9},... | collective-permute-start | bytes 786440 | tf_op jit(solution)/shard_map/ppermute | solution.py:15
  97.8 158.6 %collective-permute-start.23 = (bf16[2,32,2048]{2,1,0:T(8,128)(2,1)}, bf16[2,32,2048]{2,1,0:T(8,128)(2,1)}, u32[]{:S(2)}, u32[]{:S(2)}) collective-permute-start(bf16[2,32,2048]{2,1,0:T(8,128)(2,1)} %pad_maximum_fusion.12), channel_id=1, source_target_pairs={{5,0},{6,1},{7,2},{8,3},{9,4},{10,5},{11,6},{12,7},{13,8},{14,9},{... | collective-permute-start | bytes 786440 | tf_op jit(solution)/shard_map/ppermute | solution.py:15
  99.7 97.8 %collective-permute-start.13 = (bf16[2,32,2048]{2,1,0:T(8,128)(2,1)}, bf16[2,32,2048]{2,1,0:T(8,128)(2,1)}, u32[]{:S(2)}, u32[]{:S(2)}) collective-permute-start(bf16[2,32,2048]{2,1,0:T(8,128)(2,1)} %pad_maximum_fusion.12), channel_id=1, source_target_pairs={{0,6},{1,7},{2,8},{3,9},{4,10},{5,11},{6,12},{7,13},{8,14},{9,15},... | collective-permute-start | bytes 786440 | tf_op jit(solution)/shard_map/ppermute | solution.py:15
  106.2 88.4 %collective-permute-start.12 = (bf16[2,32,2048]{2,1,0:T(8,128)(2,1)}, bf16[2,32,2048]{2,1,0:T(8,128)(2,1)}, u32[]{:S(2)}, u32[]{:S(2)}) collective-permute-start(bf16[2,32,2048]{2,1,0:T(8,128)(2,1)} %pad_maximum_fusion.12), channel_id=1, source_target_pairs={{0,7},{1,8},{2,9},{3,10},{4,11},{5,12},{6,13},{7,14},{8,15},{16,23... | collective-permute-start | bytes 786440 | tf_op jit(solution)/shard_map/ppermute | solution.py:15
  194.6 12.9 %collective-permute-start.14 = (bf16[2,32,2048]{2,1,0:T(8,128)(2,1)}, bf16[2,32,2048]{2,1,0:T(8,128)(2,1)S(1)}, u32[]{:S(2)}, u32[]{:S(2)}) collective-permute-start(bf16[2,32,2048]{2,1,0:T(8,128)(2,1)} %pad_maximum_fusion.12), channel_id=1, source_target_pairs={{0,5},{1,6},{2,7},{3,8},{4,9},{5,10},{6,11},{7,12},{8,13},{9,14},{... | collective-permute-start | bytes 786440 | tf_op jit(solution)/shard_map/ppermute | solution.py:15
  197.5 15.5 %collective-permute-start.15 = (bf16[2,32,2048]{2,1,0:T(8,128)(2,1)}, bf16[2,32,2048]{2,1,0:T(8,128)(2,1)S(1)}, u32[]{:S(2)}, u32[]{:S(2)}) collective-permute-start(bf16[2,32,2048]{2,1,0:T(8,128)(2,1)} %pad_maximum_fusion.12), channel_id=1, source_target_pairs={{0,4},{1,5},{2,6},{3,7},{4,8},{5,9},{6,10},{7,11},{8,12},{9,13},{1... | collective-permute-start | bytes 786440 | tf_op jit(solution)/shard_map/ppermute | solution.py:15
  207.5 10.7 %collective-permute-start.16 = (bf16[2,32,2048]{2,1,0:T(8,128)(2,1)}, bf16[2,32,2048]{2,1,0:T(8,128)(2,1)S(1)}, u32[]{:S(2)}, u32[]{:S(2)}) collective-permute-start(bf16[2,32,2048]{2,1,0:T(8,128)(2,1)} %pad_maximum_fusion.12), channel_id=1, source_target_pairs={{0,3},{1,4},{2,5},{3,6},{4,7},{5,8},{6,9},{7,10},{8,11},{9,12},{10... | collective-permute-start | bytes 786440 | tf_op jit(solution)/shard_map/ppermute | solution.py:15
  223.2 16.4 %collective-permute-start.20 = (bf16[2,32,2048]{2,1,0:T(8,128)(2,1)}, bf16[2,32,2048]{2,1,0:T(8,128)(2,1)S(1)}, u32[]{:S(2)}, u32[]{:S(2)}) collective-permute-start(bf16[2,32,2048]{2,1,0:T(8,128)(2,1)} %pad_maximum_fusion.12), channel_id=1, source_target_pairs={{2,0},{3,1},{4,2},{5,3},{6,4},{7,5},{8,6},{9,7},{10,8},{11,9},{12,... | collective-permute-start | bytes 786440 | tf_op jit(solution)/shard_map/ppermute | solution.py:15
  236.1 10.7 %collective-permute-start.21 = (bf16[2,32,2048]{2,1,0:T(8,128)(2,1)}, bf16[2,32,2048]{2,1,0:T(8,128)(2,1)S(1)}, u32[]{:S(2)}, u32[]{:S(2)}) collective-permute-start(bf16[2,32,2048]{2,1,0:T(8,128)(2,1)} %pad_maximum_fusion.12), channel_id=1, source_target_pairs={{3,0},{4,1},{5,2},{6,3},{7,4},{8,5},{9,6},{10,7},{11,8},{12,9},{13... | collective-permute-start | bytes 786440 | tf_op jit(solution)/shard_map/ppermute | solution.py:15
  239.6 11.3 %collective-permute-start.22 = (bf16[2,32,2048]{2,1,0:T(8,128)(2,1)}, bf16[2,32,2048]{2,1,0:T(8,128)(2,1)S(1)}, u32[]{:S(2)}, u32[]{:S(2)}) collective-permute-start(bf16[2,32,2048]{2,1,0:T(8,128)(2,1)} %pad_maximum_fusion.12), channel_id=1, source_target_pairs={{4,0},{5,1},{6,2},{7,3},{8,4},{9,5},{10,6},{11,7},{12,8},{13,9},{1... | collective-permute-start | bytes 786440 | tf_op jit(solution)/shard_map/ppermute | solution.py:15
  246.8 66.8 %collective-permute-start.11 = (bf16[2,64,2048]{2,1,0:T(8,128)(2,1)}, bf16[2,64,2048]{2,1,0:T(8,128)(2,1)}, u32[]{:S(2)}, u32[]{:S(2)}) collective-permute-start(bf16[2,64,2048]{2,1,0:T(8,128)(2,1)} %pad_maximum_fusion.11), channel_id=1, source_target_pairs={{3,0},{4,1},{5,2},{6,3},{7,4},{8,5},{9,6},{10,7},{11,8},{12,9},{13... | collective-permute-start | bytes 1572872 | tf_op jit(solution)/shard_map/ppermute | solution.py:15
  250.9 59.2 %collective-permute-start.10 = (bf16[2,64,2048]{2,1,0:T(8,128)(2,1)}, bf16[2,64,2048]{2,1,0:T(8,128)(2,1)}, u32[]{:S(2)}, u32[]{:S(2)}) collective-permute-start(bf16[2,64,2048]{2,1,0:T(8,128)(2,1)} %pad_maximum_fusion.11), channel_id=1, source_target_pairs={{2,0},{3,1},{4,2},{5,3},{6,4},{7,5},{8,6},{9,7},{10,8},{11,9},{12,... | collective-permute-start | bytes 1572872 | tf_op jit(solution)/shard_map/ppermute | solution.py:15
  256.4 45.8 %collective-permute-start.8 = (bf16[2,64,2048]{2,1,0:T(8,128)(2,1)}, bf16[2,64,2048]{2,1,0:T(8,128)(2,1)}, u32[]{:S(2)}, u32[]{:S(2)}) collective-permute-start(bf16[2,64,2048]{2,1,0:T(8,128)(2,1)} %pad_maximum_fusion.11), channel_id=1, source_target_pairs={{0,1},{1,2},{2,3},{3,4},{4,5},{5,6},{6,7},{7,8},{8,9},{9,10},{10,1... | collective-permute-start | bytes 1572872 | tf_op jit(solution)/shard_map/ppermute | solution.py:15
  259.7 32.5 %collective-permute-start.7 = (bf16[2,64,2048]{2,1,0:T(8,128)(2,1)}, bf16[2,64,2048]{2,1,0:T(8,128)(2,1)}, u32[]{:S(2)}, u32[]{:S(2)}) collective-permute-start(bf16[2,64,2048]{2,1,0:T(8,128)(2,1)} %pad_maximum_fusion.11), channel_id=1, source_target_pairs={{0,2},{1,3},{2,4},{3,5},{4,6},{5,7},{6,8},{7,9},{8,10},{9,11},{10,... | collective-permute-start | bytes 1572872 | tf_op jit(solution)/shard_map/ppermute | solution.py:15
  263.3 25.9 %collective-permute-start.6 = (bf16[2,64,2048]{2,1,0:T(8,128)(2,1)}, bf16[2,64,2048]{2,1,0:T(8,128)(2,1)}, u32[]{:S(2)}, u32[]{:S(2)}) collective-permute-start(bf16[2,64,2048]{2,1,0:T(8,128)(2,1)} %pad_maximum_fusion.11), channel_id=1, source_target_pairs={{0,3},{1,4},{2,5},{3,6},{4,7},{5,8},{6,9},{7,10},{8,11},{9,12},{10... | collective-permute-start | bytes 1572872 | tf_op jit(solution)/shard_map/ppermute | solution.py:15
  289.2 16.3 %collective-permute-start.9 = (bf16[2,64,2048]{2,1,0:T(8,128)(2,1)}, bf16[2,64,2048]{2,1,0:T(8,128)(2,1)S(1)}, u32[]{:S(2)}, u32[]{:S(2)}) collective-permute-start(bf16[2,64,2048]{2,1,0:T(8,128)(2,1)} %pad_maximum_fusion.11), channel_id=1, source_target_pairs={{1,0},{2,1},{3,2},{4,3},{5,4},{6,5},{7,6},{8,7},{9,8},{10,9},{11,1... | collective-permute-start | bytes 1572872 | tf_op jit(solution)/shard_map/ppermute | solution.py:15
  292.2 55.3 %collective-permute-start.5 = (bf16[2,128,2048]{1,2,0:T(8,128)(2,1)}, bf16[2,128,2048]{1,2,0:T(8,128)(2,1)}, u32[]{:S(2)}, u32[]{:S(2)}) collective-permute-start(bf16[2,128,2048]{1,2,0:T(8,128)(2,1)} %pad_maximum_fusion.10), channel_id=1, source_target_pairs={{1,0},{2,1},{3,2},{4,3},{5,4},{6,5},{7,6},{8,7},{9,8},{10,9},{11,1... | collective-permute-start | bytes 3145736 | tf_op jit(solution)/shard_map/ppermute | solution.py:26
  302.2 51.4 %collective-permute-start.4 = (bf16[2,128,2048]{1,2,0:T(8,128)(2,1)}, bf16[2,128,2048]{1,2,0:T(8,128)(2,1)}, u32[]{:S(2)}, u32[]{:S(2)}) collective-permute-start(bf16[2,128,2048]{1,2,0:T(8,128)(2,1)} %pad_maximum_fusion.10), channel_id=1, source_target_pairs={{0,1},{1,2},{2,3},{3,4},{4,5},{5,6},{6,7},{7,8},{8,9},{9,10},{10,1... | collective-permute-start | bytes 3145736 | tf_op jit(solution)/shard_map/ppermute | solution.py:23
  305.5 96.6 %collective-permute-start = (bf16[2,128,2048]{2,1,0:T(8,128)(2,1)}, bf16[2,128,2048]{2,1,0:T(8,128)(2,1)}, u32[]{:S(2)}, u32[]{:S(2)}) collective-permute-start(bf16[2,128,2048]{2,1,0:T(8,128)(2,1)} %get-tuple-element.23), channel_id=1, source_target_pairs={{0,1},{1,2},{2,3},{3,4},{4,5},{5,6},{6,7},{7,8},{8,9},{9,10},{10,1... | collective-permute-start | bytes 3145736 | tf_op jit(solution)/shard_map/ppermute | solution.py:23
  310.1 65.6 %collective-permute-start.2 = (bf16[2,128,2048]{2,1,0:T(8,128)(2,1)}, bf16[2,128,2048]{2,1,0:T(8,128)(2,1)}, u32[]{:S(2)}, u32[]{:S(2)}) collective-permute-start(bf16[2,128,2048]{2,1,0:T(8,128)(2,1)} %get-tuple-element.31), channel_id=1, source_target_pairs={{0,1},{1,2},{2,3},{3,4},{4,5},{5,6},{6,7},{7,8},{8,9},{9,10},{10,1... | collective-permute-start | bytes 3145736 | tf_op jit(solution)/shard_map/ppermute | solution.py:23
  313.6 65.8 %collective-permute-start.3 = (bf16[2,128,2048]{2,1,0:T(8,128)(2,1)}, bf16[2,128,2048]{2,1,0:T(8,128)(2,1)}, u32[]{:S(2)}, u32[]{:S(2)}) collective-permute-start(bf16[2,128,2048]{2,1,0:T(8,128)(2,1)} %get-tuple-element.32), channel_id=1, source_target_pairs={{1,0},{2,1},{3,2},{4,3},{5,4},{6,5},{7,6},{8,7},{9,8},{10,9},{11,1... | collective-permute-start | bytes 3145736 | tf_op jit(solution)/shard_map/ppermute | solution.py:26
  347.5 54.6 %collective-permute-start.1 = (bf16[2,128,2048]{2,1,0:T(8,128)(2,1)}, bf16[2,128,2048]{2,1,0:T(8,128)(2,1)}, u32[]{:S(2)}, u32[]{:S(2)}) collective-permute-start(bf16[2,128,2048]{2,1,0:T(8,128)(2,1)} %get-tuple-element.24), channel_id=1, source_target_pairs={{1,0},{2,1},{3,2},{4,3},{5,4},{6,5},{7,6},{8,7},{9,8},{10,9},{11,1... | collective-permute-start | bytes 3145736 | tf_op jit(solution)/shard_map/ppermute | solution.py:26
  (39 other events, 304.6 us)
Sparse Core Ops, SparseCore 0:
  108.7 84.7 all-gather.1
where the time goes:
time: 545 us; the launch traced here: 535 us
  local copies, waits for them, and re-layouts  178 us (33%)
  other arithmetic  111 us (20%)
  starting transfers between devices  78.7 us (14%)
  waiting for transfers between devices  77 us (14%)
  matrix products  75.6 us (14%)
  between operations  15 us (3%)
    ppermute x20, starting transfers between devices, shifted(): return lax.ppermute(block, axis, route)  53.7 us
    unnamed x108, local copies, waits for them, and re-layouts  47.8 us
    dot_general x1, matrix products, per_device(): jnp.dot(attended, lax.all_gather(out_weight, 'ctx', axis=1, tiled=True),...  47.2 us
    convert_element_type x6, other arithmetic, coarsen(): matrix.reshape(matrix.shape[0] // 2, 2, matrix.shape[1]).astype(jnp.float32)  44.8 us
    convert_element_type x15, local copies, waits for them, and re-layouts, coarsen(): matrix.reshape(matrix.shape[0] // 2, 2, matrix.shape[1]).astype(jnp.float32)  42.1 us
    ppermute x20, waiting for transfers between devices, shifted(): return lax.ppermute(block, axis, route)  39.6 us
    convert_element_type x6, other arithmetic, coarsen(): return ((paired[:, 0] + paired[:, 1]) * 0.5).astype(jnp.bfloat16)  21.3 us
    ppermute x3, waiting for transfers between devices, padded(): lax.ppermute(lax.slice_in_dim(block, block.shape[dim] - width, None, axis...  19.8 us
  transfers between devices with their start and end apart: 27, of which 10 were waited for; matrix products, arithmetic and copies ran while one was open for 38% of the time, Pallas kernels for 0%

commit v1 on v0

v1 whole, which is shorter than its diff:
```python
import math

import jax
import jax.numpy as jnp
from jax import lax
from jax.experimental import pallas as pl
from jax.experimental.pallas import tpu as pltpu
from jax.sharding import PartitionSpec as P

HEAD_DIM = 128
BLOCK = 128
HALF = BLOCK // 2
LOG2 = HEAD_DIM**-0.5 * math.log2(math.e)
MASKED = -1e30
BF16 = jnp.bfloat16
F32 = jnp.float32


def halved(ref, start, rows):
    even = ref[pl.ds(start, rows, stride=2), :]
    odd = ref[pl.ds(start + 1, rows, stride=2), :]
    return ((even + odd) * 0.5).astype(BF16)


def prepare_kernel(info, k_ref, v_ref, x_ref, s_ref, l3_ref, l4_ref, fine):
    odd_core = info[0] == 1
    for side, source in enumerate((k_ref, v_ref)):
        fine[...] = source[...].astype(F32)
        one = halved(fine, 0, 256)
        fine[0:256, :] = one.astype(F32)
        two = halved(fine, 0, 128)
        fine[0:128, :] = two.astype(F32)
        three = halved(fine, 0, 64)
        l3_ref[side] = three
        fine[0:64, :] = three.astype(F32)
        l4_ref[side] = halved(fine, 0, 32)

        def put(low_ref, high_ref):
            low_ref[side, 0:128, :] = source[0:128, :]
            low_ref[side, 128:192, :] = one[64:128]
            low_ref[side, 192:256, :] = two[64:128]
            high_ref[side, 0:128, :] = source[384:512, :]
            high_ref[side, 128:192, :] = one[128:192]
            high_ref[side, 192:256, :] = two[0:64]

        @pl.when(odd_core)
        def _():
            put(s_ref, x_ref)

        @pl.when(jnp.logical_not(odd_core))
        def _():
            put(x_ref, s_ref)


def prepare(info, keys, values):
    rows, channels = keys.shape
    column = pl.BlockSpec((rows, HEAD_DIM), lambda h, info: (0, h))

    def out(n):
        return pl.BlockSpec((2, n, HEAD_DIM), lambda h, info: (0, 0, h))

    def shape(n):
        return jax.ShapeDtypeStruct((2, n, channels), BF16)

    return pl.pallas_call(
        prepare_kernel,
        grid_spec=pltpu.PrefetchScalarGridSpec(
            num_scalar_prefetch=1,
            grid=(channels // HEAD_DIM,),
            in_specs=[column, column],
            out_specs=[out(256), out(256), out(64), out(32)],
            scratch_shapes=[pltpu.VMEM((rows, HEAD_DIM), F32)],
        ),
        out_shape=[shape(256), shape(256), shape(64), shape(32)],
        name="prepare",
    )(info, keys, values)


def third_kernel(info, x_ref, o_ref, fine):
    odd_core = info[0] == 1
    for side in range(2):
        fine[0:128, :] = x_ref[side, 0:128, :].astype(F32)
        one = halved(fine, 0, 64).astype(F32)
        sent_one = x_ref[side, 128:192, :].astype(F32)
        fine[0:64, :] = jnp.where(odd_core, one, sent_one)
        fine[64:128, :] = jnp.where(odd_core, sent_one, one)
        two = halved(fine, 0, 64).astype(F32)
        sent_two = x_ref[side, 192:256, :].astype(F32)
        fine[0:64, :] = jnp.where(odd_core, two, sent_two)
        fine[64:128, :] = jnp.where(odd_core, sent_two, two)
        o_ref[side] = halved(fine, 0, 64)


def third(info, x_halo):
    channels = x_halo.shape[2]
    return pl.pallas_call(
        third_kernel,
        grid_spec=pltpu.PrefetchScalarGridSpec(
            num_scalar_prefetch=1,
            grid=(channels // HEAD_DIM,),
            in_specs=[pl.BlockSpec((2, 256, HEAD_DIM), lambda h, info: (0, 0, h))],
            out_specs=pl.BlockSpec((2, 64, HEAD_DIM), lambda h, info: (0, 0, h)),
            scratch_shapes=[pltpu.VMEM((128, HEAD_DIM), F32)],
        ),
        out_shape=jax.ShapeDtypeStruct((2, 64, channels), BF16),
        name="third",
    )(info, x_halo)


def softmax_block(queries, keys, values, bias=None):
    scores = lax.dot_general(
        queries, keys, (((1,), (1,)), ((), ())), preferred_element_type=F32
    )
    if bias is not None:
        scores = scores + bias
    peak = jnp.max(scores, axis=1, keepdims=True)
    weights = jnp.exp2((scores - peak) * LOG2).astype(BF16)
    both = jnp.dot(weights, values, preferred_element_type=F32)
    peak = jnp.broadcast_to(peak, (peak.shape[0], HEAD_DIM))
    return peak, both[:, :HEAD_DIM], both[:, HEAD_DIM:]


def attend_kernel(
    info, q_ref, k_ref, v_ref, x_ref, s_ref, a_ref, u_ref, d_ref, g_ref, w_ref, o_ref,
    fine, halo, q1, q2, q3, q4, k0, v0, k1, v1, k2, v2, k3, v3, k4, v4, um, uu, uz,
):
    odd_core = info[0] == 1

    @pl.when(pl.program_id(0) == 0)
    def _():
        for ref in (v0, v1, v2, v3, v4):
            ref[:, HEAD_DIM:] = jnp.ones((ref.shape[0], HEAD_DIM), BF16)

    fine[...] = q_ref[...].astype(F32)
    q1[...] = halved(fine, 0, 256)
    fine[0:256, :] = q1[...].astype(F32)
    q2[...] = halved(fine, 0, 128)
    fine[0:128, :] = q2[...].astype(F32)
    q3[...] = halved(fine, 0, 64)
    fine[0:64, :] = q3[...].astype(F32)
    q4[...] = halved(fine, 0, 32)

    for side, (own, z0, z1, z2, z3, z4) in enumerate(
        ((k_ref, k0, k1, k2, k3, k4), (v_ref, v0, v1, v2, v3, v4))
    ):
        lanes = slice(0, HEAD_DIM)
        z0[128:640, lanes] = own[...]
        fine[...] = own[...].astype(F32)
        one = halved(fine, 0, 256)
        z1[0:128, lanes] = one[128:256]
        z1[384:512, lanes] = one[0:128]

        def place(left_ref, right_ref):
            z0[0:128, lanes] = left_ref[side, 0:128, :]
            z0[640:768, lanes] = right_ref[side, 0:128, :]
            halo[0:128, :] = left_ref[side, 0:128, :].astype(F32)
            left_one = halved(halo, 0, 64)
            z1[128:192, lanes] = left_ref[side, 128:192, :]
            z1[192:256, lanes] = left_one
            halo[0:64, :] = left_ref[side, 128:192, :].astype(F32)
            halo[64:128, :] = left_one.astype(F32)
            z2[128:192, lanes] = left_ref[side, 192:256, :]
            z2[192:256, lanes] = halved(halo, 0, 64)
            halo[0:128, :] = right_ref[side, 0:128, :].astype(F32)
            right_one = halved(halo, 0, 64)
            z1[256:320, lanes] = right_one
            z1[320:384, lanes] = right_ref[side, 128:192, :]
            halo[0:64, :] = right_one.astype(F32)
            halo[64:128, :] = right_ref[side, 128:192, :].astype(F32)
            z2[0:64, lanes] = halved(halo, 0, 64)
            z2[64:128, lanes] = right_ref[side, 192:256, :]

        @pl.when(odd_core)
        def _():
            place(s_ref, x_ref)

        @pl.when(jnp.logical_not(odd_core))
        def _():
            place(x_ref, s_ref)

        z3[0:64, lanes] = a_ref[side]
        z3[64:192, lanes] = w_ref[side, 0:128, :]
        z4[0:32, lanes] = u_ref[side]
        z4[32:64, lanes] = d_ref[side]
        z4[64:96, lanes] = g_ref[side]
        z4[96:192, lanes] = w_ref[side, 128:224, :]

    def bias_of(flag):
        return jnp.where(info[flag] == 1, 0.0, MASKED).astype(F32)

    lane = lax.broadcasted_iota(jnp.int32, (1, 192), 1)
    wide = lax.broadcasted_iota(jnp.int32, (1, 384), 1)
    left0, right0 = bias_of(2), bias_of(3)
    first0 = jnp.where(wide < 128, left0, 0.0)
    last0 = jnp.where(wide >= 256, right0, 0.0)

    b4 = lane % 96
    l4, r4, g4 = bias_of(6), bias_of(7), bias_of(8)
    bias4 = jnp.where(b4 < 32, l4, jnp.where(b4 < 64, r4, g4))
    peak, num, den = softmax_block(q4[...], k4[...], v4[...], bias4)

    def widened(level_peak, level_num, level_den, acc, rows):
        for ref, value in zip((um, uu, uz), acc, strict=True):
            ref[pl.ds(0, rows // 2, stride=2), :] = value
            ref[pl.ds(1, rows // 2, stride=2), :] = value
        high = jnp.maximum(level_peak, um[0:rows, :])
        here = jnp.exp2((level_peak - high) * LOG2)
        there = 2.0 * jnp.exp2((um[0:rows, :] - high) * LOG2)
        return (
            high,
            here * level_num + there * uu[0:rows, :],
            here * level_den + there * uz[0:rows, :],
        )

    bias3 = jnp.where(lane < 64, bias_of(4), bias_of(5))
    acc = widened(*softmax_block(q3[...], k3[...], v3[...], bias3), (peak, num, den), 64)

    def stacked(parts):
        return tuple(jnp.concatenate(part, axis=0) for part in zip(*parts, strict=True))

    low2 = jnp.where(lane < 128, right0, left0)
    high2 = jnp.where(lane < 64, right0, left0)
    level = stacked(
        [
            softmax_block(q2[0:64, :], k2[0:192, :], v2[0:192, :], low2),
            softmax_block(q2[64:128, :], k2[64:256, :], v2[64:256, :], high2),
        ]
    )
    acc = widened(*level, acc, 128)

    first_low = jnp.where(lane < 128, 0.0, left0)
    first_high = jnp.where(lane < 64, 0.0, left0)
    last_low = jnp.where(lane < 128, right0, 0.0)
    last_high = jnp.where(lane < 64, right0, 0.0)
    level = stacked(
        [
            softmax_block(q1[0:64, :], k1[0:192, :], v1[0:192, :], first_low),
            softmax_block(q1[64:128, :], k1[64:256, :], v1[64:256, :], first_high),
            softmax_block(q1[128:192, :], k1[256:448, :], v1[256:448, :], last_low),
            softmax_block(q1[192:256, :], k1[320:512, :], v1[320:512, :], last_high),
        ]
    )
    acc = widened(*level, acc, 256)

    for ref, value in zip((um, uu, uz), acc, strict=True):
        ref[pl.ds(0, 256, stride=2), :] = value
        ref[pl.ds(1, 256, stride=2), :] = value
    for block in range(4):
        rows = slice(block * 128, block * 128 + 128)
        window = slice(block * 128, block * 128 + 384)
        bias = first0 if block == 0 else last0 if block == 3 else None
        peak, num, den = softmax_block(q_ref[rows, :], k0[window, :], v0[window, :], bias)
        coarse = um[rows, :]
        high = jnp.maximum(peak, coarse)
        here = jnp.exp2((peak - high) * LOG2)
        there = 2.0 * jnp.exp2((coarse - high) * LOG2)
        total = here * num + there * uu[rows, :]
        norm = here * den + there * uz[rows, :]
        o_ref[rows, :] = (total / norm).astype(BF16)


def attend(info, queries, keys, values, x_halo, s_halo, a, u, d, g, swapped):
    rows, channels = queries.shape
    column = pl.BlockSpec((rows, HEAD_DIM), lambda h, info: (0, h))

    def pair(n):
        return pl.BlockSpec((2, n, HEAD_DIM), lambda h, info: (0, 0, h))

    def k(n):
        return pltpu.VMEM((n, HEAD_DIM), BF16)

    def v(n):
        return pltpu.VMEM((n, 2 * HEAD_DIM), BF16)

    def f(n):
        return pltpu.VMEM((n, HEAD_DIM), F32)

    return pl.pallas_call(
        attend_kernel,
        grid_spec=pltpu.PrefetchScalarGridSpec(
            num_scalar_prefetch=1,
            grid=(channels // HEAD_DIM,),
            in_specs=[column, column, column, pair(256), pair(256), pair(64)]
            + [pair(32), pair(32), pair(32), pair(224)],
            out_specs=column,
            scratch_shapes=[f(512), f(128), k(256), k(128), k(64), k(32)]
            + [k(768), v(768), k(512), v(512), k(256), v(256), k(192), v(192), k(192), v(192)]
            + [f(512), f(512), f(512)],
        ),
        out_shape=jax.ShapeDtypeStruct((rows, channels), BF16),
        name="attend",
    )(info, queries, keys, values, x_halo, s_halo, a, u, d, g, swapped)


def project_kernel(a_ref, w_ref, o_ref):
    weight = jnp.concatenate([w_ref[i] for i in range(w_ref.shape[0])], axis=1)
    o_ref[...] = jnp.dot(a_ref[...], weight, preferred_element_type=F32).astype(BF16)


def project(attended, weight):
    rows, channels = attended.shape
    count, _, width = weight.shape
    step = 4
    return pl.pallas_call(
        project_kernel,
        grid=(count // step,),
        in_specs=[
            pl.BlockSpec((rows, channels), lambda j: (0, 0)),
            pl.BlockSpec((step, channels, width), lambda j: (j, 0, 0)),
        ],
        out_specs=pl.BlockSpec((rows, step * width), lambda j: (0, j)),
        out_shape=jax.ShapeDtypeStruct((rows, count * width), BF16),
        name="project",
    )(attended, weight)


def permuted(block, target):
    n = lax.axis_size("ctx")
    route = [(d, target(d)) for d in range(n) if 0 <= target(d) < n]
    return lax.ppermute(block, "ctx", route)


def per_device(queries, keys, values, out_weight):
    n = lax.axis_size("ctx")
    d = lax.axis_index("ctx")
    core, chip_odd = d % 2, (d // 2) % 2
    left3, right3 = d >= 2, d < n - 2
    left4, right4 = d >= 4, d < n - 4
    info = jnp.stack(
        [
            core,
            chip_odd,
            (d > 0).astype(jnp.int32),
            (d < n - 1).astype(jnp.int32),
            jnp.where(core == 1, right3, left3).astype(jnp.int32),
            jnp.where(core == 1, left3, right3).astype(jnp.int32),
            left4.astype(jnp.int32),
            right4.astype(jnp.int32),
            jnp.where(chip_odd == 1, left4, right4).astype(jnp.int32),
        ]
    )
    x_send, s_send, l3, l4 = prepare(info, keys, values)
    x_halo = permuted(x_send, lambda i: i + 1 if i % 2 else i - 1)
    s_halo = permuted(s_send, lambda i: i ^ 1)
    a = permuted(l3, lambda i: i - 2 if i % 2 else i + 2)
    up = permuted(l4, lambda i: i + 4)
    down = permuted(l4, lambda i: i - 4)
    diagonal = permuted(l4, lambda i: i - 6 if (i // 2) % 2 else i + 6)
    neighbour3 = third(info, x_halo)
    swapped = permuted(
        jnp.concatenate([a, neighbour3, up, down, diagonal], axis=1), lambda i: i ^ 1
    )
    attended = attend(
        info, queries, keys, values, x_halo, s_halo, a, up, down, diagonal, swapped
    )
    width = out_weight.shape[1]
    if width % 128 == 0:
        weight = lax.all_gather(out_weight, "ctx", axis=0)
    else:
        weight = lax.all_gather(out_weight, "ctx", axis=1, tiled=True)
        weight = weight.reshape(weight.shape[0], -1, 128).transpose(1, 0, 2)
    return project(attended, weight)


def solution(mesh):
    rows = P(("groups", "ctx"), None)
    return jax.shard_map(
        per_device,
        mesh=mesh,
        in_specs=(rows, rows, rows, P(None, "ctx")),
        out_specs=rows,
        check_vma=False,
    )
```

time: 545 us -> 201 us (0.37); the launches traced: 535 us -> 199 us
  local copies, waits for them, and re-layouts: 178 us -> 8.25 us
  other arithmetic: 111 us -> 0 us
  Pallas kernels: 0 us -> 83.3 us
  matrix products: 75.6 us -> 0 us
  starting transfers between devices: 78.7 us -> 15.9 us
    pallas_call x0 -> x4, Pallas kernels: none -> 83.3 us  [the longest x1 51.8 us: attend(): pl.pallas_call(attend_kernel, grid_spec=pltpu.PrefetchScalarGridSpec(num_...]
    dot_general x11 -> x0, matrix products: 75.6 us -> none  [the longest x1 47.2 us: per_device(): jnp.dot(attended, lax.all_gather(out_weight, 'ctx', axis=1, tiled=True),...]
    convert_element_type x12 -> x0, other arithmetic: 66.1 us -> none  [the longest x6 44.8 us: coarsen(): matrix.reshape(matrix.shape[0] // 2, 2, matrix.shape[1]).astype(jnp.float32)]
    ppermute x26 -> x7, starting transfers between devices: 78.7 us -> 15.9 us  [permuted(): return lax.ppermute(block, 'ctx', route)]
    convert_element_type x15 -> x0, local copies, waits for them, and re-layouts: 42.1 us -> none  [coarsen(): matrix.reshape(matrix.shape[0] // 2, 2, matrix.shape[1]).astype(jnp.float32)]
    unnamed x108 -> x16, local copies, waits for them, and re-layouts: 47.8 us -> 6.88 us
    reshape x27 -> x0, local copies, waits for them, and re-layouts: 23 us -> none  [the longest x4 7.41 us: per_device(): parts_list.append(right_keys.reshape(grouped))]
    slice x6 -> x0, local copies, waits for them, and re-layouts: 19.3 us -> none  [coarsen(): return ((paired[:, 0] + paired[:, 1]) * 0.5).astype(jnp.bfloat16)]
  transfers between devices with their start and end apart: 27 -> 8, of which waited for: 10 -> 3; matrix products, arithmetic and copies ran while one was open for 38% -> 3% of each run, Pallas kernels for 0% -> 37%
where the time goes in v1:
time: 201 us; the launch traced here: 199 us
  Pallas kernels  83.3 us (41%)
  waiting for transfers between devices  78 us (39%)
  starting transfers between devices  15.9 us (8%)
  between operations  13.5 us (7%)
  local copies, waits for them, and re-layouts  8.25 us (4%)
    ppermute x7, waiting for transfers between devices, permuted(): return lax.ppermute(block, 'ctx', route)  77.2 us
    pallas_call x1, Pallas kernels, attend(): pl.pallas_call(attend_kernel, grid_spec=pltpu.PrefetchScalarGridSpec(num_...  51.8 us
    ppermute x7, starting transfers between devices, permuted(): return lax.ppermute(block, 'ctx', route)  15.9 us
    pallas_call x1, Pallas kernels, prepare(): pl.pallas_call(prepare_kernel, grid_spec=pltpu.PrefetchScalarGridSpec(num...  12.4 us
    pallas_call x1, Pallas kernels, third(): pl.pallas_call(third_kernel, grid_spec=pltpu.PrefetchScalarGridSpec(num_s...  10.3 us
    pallas_call x1, Pallas kernels, project(): pl.pallas_call(project_kernel, grid=(count // step,), in_specs=[pl.BlockS...  8.72 us
    unnamed x16, local copies, waits for them, and re-layouts  6.88 us
  transfers between devices with their start and end apart: 8, of which 3 were waited for; matrix products, arithmetic and copies ran while one was open for 3% of the time, Pallas kernels for 37%

profile of v1, /device:TPU:10, one launch (start us, length us, event | category | flops | bytes accessed | tf_op | source)
XLA Modules:
  0.0 198.9 jit_solution(6283284298208684140)
XLA Ops:
  6.5 0.7 all-gather.3.cloned.1.call-update
  7.3 0.6 stack.67.info
  7.9 12.4 %prepare.1 = (bf16[2,256,2048]{2,1,0:T(8,128)(2,1)}, bf16[2,256,2048]{2,1,0:T(8,128)(2,1)}, bf16[2,64,2048]{2,1,0:T(8,128)(2,1)}, bf16[2,32,2048]{2,1,0:T(8,128)(2,1)}) custom-call(s32[9]{0:T(128)} %stack.67.info, bf16[512,2048]{1,0:T(8,128)(2,1)} %k_ref.3, bf16[512,2048]{1,0:T(8,128)(2,1)} %v_ref.3), custom_call_target="tpu_custom_call" | custom-call | tf_op jit(solution)/shard_map/prepare/pallas_call | solution.py:65
  20.3 1.9 collective-permute-start
  22.3 4.1 %collective-permute-start.2 = (bf16[2,64,2048]{2,1,0:T(8,128)(2,1)}, bf16[2,64,2048]{2,1,0:T(8,128)(2,1)S(1)}, u32[]{:S(2)}, u32[]{:S(2)}) collective-permute-start(bf16[2,64,2048]{2,1,0:T(8,128)(2,1)} %get-tuple-element.11), channel_id=1, source_target_pairs={{0,2},{2,4},{3,1},{4,6},{5,3},{6,8},{7,5},{8,10},{9,7},{10,12},{11... | collective-permute-start | bytes 1572872 | tf_op jit(solution)/shard_map/ppermute | solution.py:320
  26.4 3.5 %collective-permute-start.3 = (bf16[2,32,2048]{2,1,0:T(8,128)(2,1)}, bf16[2,32,2048]{2,1,0:T(8,128)(2,1)S(1)}, u32[]{:S(2)}, u32[]{:S(2)}) collective-permute-start(bf16[2,32,2048]{2,1,0:T(8,128)(2,1)} %get-tuple-element.12), channel_id=1, source_target_pairs={{0,4},{1,5},{2,6},{3,7},{4,8},{5,9},{6,10},{7,11},{8,12},{9,13},{1... | collective-permute-start | bytes 786440 | tf_op jit(solution)/shard_map/ppermute | solution.py:320
  29.9 2.4 %collective-permute-start.4 = (bf16[2,32,2048]{2,1,0:T(8,128)(2,1)}, bf16[2,32,2048]{2,1,0:T(8,128)(2,1)S(1)}, u32[]{:S(2)}, u32[]{:S(2)}) collective-permute-start(bf16[2,32,2048]{2,1,0:T(8,128)(2,1)} %get-tuple-element.12), channel_id=1, source_target_pairs={{4,0},{5,1},{6,2},{7,3},{8,4},{9,5},{10,6},{11,7},{12,8},{13,9},{1... | collective-permute-start | bytes 786440 | tf_op jit(solution)/shard_map/ppermute | solution.py:320
  32.2 1.9 collective-permute-start.5
  34.2 25.8 %collective-permute-done.2.a_ref = bf16[2,64,2048]{2,1,0:T(8,128)(2,1)S(1)} collective-permute-done((bf16[2,64,2048]{2,1,0:T(8,128)(2,1)}, bf16[2,64,2048]{2,1,0:T(8,128)(2,1)S(1)}, u32[]{:S(2)}, u32[]{:S(2)}) %collective-permute-start.2) | collective-permute-done | bytes 524320 | tf_op jit(solution)/shard_map/ppermute | solution.py:320
  60.0 2.1 %collective-permute-start.1 = (bf16[2,256,2048]{2,1,0:T(8,128)(2,1)}, bf16[2,256,2048]{2,1,0:T(8,128)(2,1)}, u32[]{:S(2)}, u32[]{:S(2)}) collective-permute-start(bf16[2,256,2048]{2,1,0:T(8,128)(2,1)} %get-tuple-element.10), channel_id=1, source_target_pairs={{0,1},{1,0},{2,3},{3,2},{4,5},{5,4},{6,7},{7,6},{8,9},{9,8},{10,11... | collective-permute-start | bytes 6291464 | tf_op jit(solution)/shard_map/ppermute | solution.py:320
  62.1 0.9 constant_dynamic-update-slice_fusion.4
  63.0 47.4 %collective-permute-done.x_ref = bf16[2,256,2048]{2,1,0:T(8,128)(2,1)S(1)} collective-permute-done((bf16[2,256,2048]{2,1,0:T(8,128)(2,1)}, bf16[2,256,2048]{2,1,0:T(8,128)(2,1)S(1)}, u32[]{:S(2)}, u32[]{:S(2)}) %collective-permute-start) | collective-permute-done | bytes 2097184 | tf_op jit(solution)/shard_map/ppermute | solution.py:320
  110.4 1.3 copy-done
  111.7 10.3 %third.1 = bf16[2,64,2048]{2,1,0:T(8,128)(2,1)} custom-call(s32[9]{0:T(128)} %stack.67.info, bf16[2,256,2048]{2,1,0:T(8,128)(2,1)} %copy-done), custom_call_target="tpu_custom_call" | custom-call | tf_op jit(solution)/shard_map/third/pallas_call | solution.py:96
  122.0 1.9 constant_dynamic-update-slice_fusion.3
  123.9 0.0 collective-permute-done.3.u_ref
  123.9 0.8 constant_dynamic-update-slice_fusion.2
  124.7 0.8 constant_dynamic-update-slice_fusion.1
  125.5 0.8 constant_dynamic-update-slice_fusion
  126.3 4.0 %collective-permute-done.6.w_ref = bf16[2,224,2048]{2,1,0:T(8,128)(2,1)S(1)} collective-permute-done((bf16[2,224,2048]{2,1,0:T(8,128)(2,1)}, bf16[2,224,2048]{2,1,0:T(8,128)(2,1)S(1)}, u32[]{:S(2)}, u32[]{:S(2)}) %collective-permute-start.6) | collective-permute-done | bytes 1835040 | tf_op jit(solution)/shard_map/ppermute | solution.py:320
  130.3 1.2 copy-done.2
  131.6 51.8 %attend.1.a_ref = bf16[512,2048]{1,0:T(8,128)(2,1)} custom-call(s32[9]{0:T(128)} %stack.67.info, bf16[512,2048]{1,0:T(8,128)(2,1)} %q_ref.1, bf16[512,2048]{1,0:T(8,128)(2,1)} %k_ref.3, bf16[512,2048]{1,0:T(8,128)(2,1)} %v_ref.3, bf16[2,256,2048]{2,1,0:T(8,128)(2,1)} %copy-done, bf16[2,256,2048]{2,1,0:T(8,128)(2,1)} %collective-permute-done.1.s_ref, ...), custom_call_target="tpu_custom_call" | custom-call | tf_op jit(solution)/shard_map/attend/pallas_call | solution.py:278
  183.3 0.0 all-gather.3.cloned.1.call-done
  183.3 8.7 %project.1 = bf16[512,2048]{1,0:T(8,128)(2,1)} custom-call(bf16[512,2048]{1,0:T(8,128)(2,1)} %attend.1.a_ref, bf16[16,2048,128]{2,1,0:T(8,128)(2,1)} %bitcast.10), custom_call_target="tpu_custom_call" | custom-call | tf_op jit(solution)/shard_map/project/pallas_call | solution.py:304
  (15 shorter events, 0.0 us)
Async XLA Ops:
  6.5 176.8 %all-gather.3.cloned.1.call-start = ((), (), s32[]{:S(2)}) async-start(), calls=%async_computation | async-start | bytes 8912896 | tf_op jit(solution)/shard_map/all_gather | solution.py:358
  20.3 90.0 %collective-permute-start = (bf16[2,256,2048]{2,1,0:T(8,128)(2,1)}, bf16[2,256,2048]{2,1,0:T(8,128)(2,1)S(1)}, u32[]{:S(2)}, u32[]{:S(2)}) collective-permute-start(bf16[2,256,2048]{2,1,0:T(8,128)(2,1)} %get-tuple-element.9), channel_id=1, source_target_pairs={{1,2},{2,1},{3,4},{4,3},{5,6},{6,5},{7,8},{8,7},{9,10},{10,9},{11,... | collective-permute-start | bytes 6291464 | tf_op jit(solution)/shard_map/ppermute | solution.py:320
  22.3 37.7 %collective-permute-start.2 = (bf16[2,64,2048]{2,1,0:T(8,128)(2,1)}, bf16[2,64,2048]{2,1,0:T(8,128)(2,1)S(1)}, u32[]{:S(2)}, u32[]{:S(2)}) collective-permute-start(bf16[2,64,2048]{2,1,0:T(8,128)(2,1)} %get-tuple-element.11), channel_id=1, source_target_pairs={{0,2},{2,4},{3,1},{4,6},{5,3},{6,8},{7,5},{8,10},{9,7},{10,12},{11... | collective-permute-start | bytes 1572872 | tf_op jit(solution)/shard_map/ppermute | solution.py:320
  26.4 97.6 %collective-permute-start.3 = (bf16[2,32,2048]{2,1,0:T(8,128)(2,1)}, bf16[2,32,2048]{2,1,0:T(8,128)(2,1)S(1)}, u32[]{:S(2)}, u32[]{:S(2)}) collective-permute-start(bf16[2,32,2048]{2,1,0:T(8,128)(2,1)} %get-tuple-element.12), channel_id=1, source_target_pairs={{0,4},{1,5},{2,6},{3,7},{4,8},{5,9},{6,10},{7,11},{8,12},{9,13},{1... | collective-permute-start | bytes 786440 | tf_op jit(solution)/shard_map/ppermute | solution.py:320
  29.9 94.9 %collective-permute-start.4 = (bf16[2,32,2048]{2,1,0:T(8,128)(2,1)}, bf16[2,32,2048]{2,1,0:T(8,128)(2,1)S(1)}, u32[]{:S(2)}, u32[]{:S(2)}) collective-permute-start(bf16[2,32,2048]{2,1,0:T(8,128)(2,1)} %get-tuple-element.12), channel_id=1, source_target_pairs={{4,0},{5,1},{6,2},{7,3},{8,4},{9,5},{10,6},{11,7},{12,8},{13,9},{1... | collective-permute-start | bytes 786440 | tf_op jit(solution)/shard_map/ppermute | solution.py:320
  32.2 93.3 %collective-permute-start.5 = (bf16[2,32,2048]{2,1,0:T(8,128)(2,1)}, bf16[2,32,2048]{2,1,0:T(8,128)(2,1)S(1)}, u32[]{:S(2)}, u32[]{:S(2)}) collective-permute-start(bf16[2,32,2048]{2,1,0:T(8,128)(2,1)} %get-tuple-element.12), channel_id=1, source_target_pairs={{0,6},{1,7},{4,10},{5,11},{6,0},{7,1},{8,14},{9,15},{10,4},{11,5},... | collective-permute-start | bytes 786440 | tf_op jit(solution)/shard_map/ppermute | solution.py:320
  60.0 62.0 %copy-start.1 = (bf16[2,64,2048]{2,1,0:T(8,128)(2,1)}, bf16[2,64,2048]{2,1,0:T(8,128)(2,1)S(1)}, u32[]{:S(2)}) copy-start(bf16[2,64,2048]{2,1,0:T(8,128)(2,1)S(1)} %collective-permute-done.2.a_ref) | copy-start | bytes 1572868
  60.0 66.3 %collective-permute-start.1 = (bf16[2,256,2048]{2,1,0:T(8,128)(2,1)}, bf16[2,256,2048]{2,1,0:T(8,128)(2,1)}, u32[]{:S(2)}, u32[]{:S(2)}) collective-permute-start(bf16[2,256,2048]{2,1,0:T(8,128)(2,1)} %get-tuple-element.10), channel_id=1, source_target_pairs={{0,1},{1,0},{2,3},{3,2},{4,5},{5,4},{6,7},{7,6},{8,9},{9,8},{10,11... | collective-permute-start | bytes 6291464 | tf_op jit(solution)/shard_map/ppermute | solution.py:320
  110.4 1.3 copy-start
  123.9 6.3 %copy-start.3 = (bf16[2,32,2048]{2,1,0:T(8,128)(2,1)}, bf16[2,32,2048]{2,1,0:T(8,128)(2,1)S(1)}, u32[]{:S(2)}) copy-start(bf16[2,32,2048]{2,1,0:T(8,128)(2,1)S(1)} %collective-permute-done.3.u_ref) | copy-start | bytes 786436
  124.7 5.6 %copy-start.4 = (bf16[2,32,2048]{2,1,0:T(8,128)(2,1)}, bf16[2,32,2048]{2,1,0:T(8,128)(2,1)S(1)}, u32[]{:S(2)}) copy-start(bf16[2,32,2048]{2,1,0:T(8,128)(2,1)S(1)} %collective-permute-done.4.d_ref) | copy-start | bytes 786436
  125.5 4.8 %copy-start.5 = (bf16[2,32,2048]{2,1,0:T(8,128)(2,1)}, bf16[2,32,2048]{2,1,0:T(8,128)(2,1)S(1)}, u32[]{:S(2)}) copy-start(bf16[2,32,2048]{2,1,0:T(8,128)(2,1)S(1)} %collective-permute-done.5.g_ref) | copy-start | bytes 786436
  126.3 4.0 %collective-permute-start.6 = (bf16[2,224,2048]{2,1,0:T(8,128)(2,1)}, bf16[2,224,2048]{2,1,0:T(8,128)(2,1)S(1)}, u32[]{:S(2)}, u32[]{:S(2)}) collective-permute-start(bf16[2,224,2048]{2,1,0:T(8,128)(2,1)} %constant_dynamic-update-slice_fusion), channel_id=1, source_target_pairs={{0,1},{1,0},{2,3},{3,2},{4,5},{5,4},{6,7},{7,6},{8,9},{9,8},{10,11... | collective-permute-start | bytes 5505032 | tf_op jit(solution)/shard_map/ppermute | solution.py:320
  130.3 1.3 copy-start.2
Sparse Core Ops, SparseCore 0:
  9.5 108.5 all-gather.2

commit v2 on v1

v2 whole, which is shorter than its diff:
```python
import math

import jax
import jax.numpy as jnp
from jax import lax
from jax.experimental import pallas as pl
from jax.experimental.pallas import tpu as pltpu
from jax.sharding import Mesh
from jax.sharding import PartitionSpec as P

HEAD_DIM = 128
BLOCK = 128
HALF = BLOCK // 2
LOG2 = HEAD_DIM**-0.5 * math.log2(math.e)
MASKED = -1e30
BF16 = jnp.bfloat16
F32 = jnp.float32


def halved(ref, start, rows):
    even = ref[pl.ds(start, rows, stride=2), :]
    odd = ref[pl.ds(start + 1, rows, stride=2), :]
    return ((even + odd) * 0.5).astype(BF16)


def prepare_kernel(info, k_ref, v_ref, x_ref, s_ref, one_ref, l3_ref, l4_ref, *scratch):
    odd_core = info[0] == 1
    columns = k_ref.shape[1] // HEAD_DIM
    work = [
        (side, slice(j * HEAD_DIM, (j + 1) * HEAD_DIM), scratch[side * columns + j])
        for side in range(2)
        for j in range(columns)
    ]
    sources = (k_ref, v_ref)
    for side, lanes, fine in work:
        fine[...] = sources[side][:, lanes].astype(F32)
    ones, twos = [], []
    for side, lanes, fine in work:
        ones.append(halved(fine, 0, 256))
        one_ref[side, :, lanes] = ones[-1]
    for (side, lanes, fine), one in zip(work, ones, strict=True):
        fine[0:256, :] = one.astype(F32)
    for side, lanes, fine in work:
        twos.append(halved(fine, 0, 128))
    for (side, lanes, fine), two in zip(work, twos, strict=True):
        fine[0:128, :] = two.astype(F32)
    for side, lanes, fine in work:
        three = halved(fine, 0, 64)
        l3_ref[side, :, lanes] = three
        fine[128:192, :] = three.astype(F32)
    for side, lanes, fine in work:
        l4_ref[side, :, lanes] = halved(fine, 128, 32)

    def put(low_ref, high_ref):
        for (side, lanes, _), one, two in zip(work, ones, twos, strict=True):
            low_ref[side, 0:128, lanes] = sources[side][0:128, lanes]
            low_ref[side, 128:192, lanes] = one[64:128]
            low_ref[side, 192:256, lanes] = two[64:128]
            high_ref[side, 0:128, lanes] = sources[side][384:512, lanes]
            high_ref[side, 128:192, lanes] = one[128:192]
            high_ref[side, 192:256, lanes] = two[0:64]

    @pl.when(odd_core)
    def _():
        put(s_ref, x_ref)

    @pl.when(jnp.logical_not(odd_core))
    def _():
        put(x_ref, s_ref)


def prepare(info, keys, values):
    rows, channels = keys.shape
    wide = 4 * HEAD_DIM
    column = pl.BlockSpec((rows, wide), lambda h, info: (0, h))

    def out(n):
        return pl.BlockSpec((2, n, wide), lambda h, info: (0, 0, h))

    def shape(n):
        return jax.ShapeDtypeStruct((2, n, channels), BF16)

    sizes = (256, 256, 256, 64, 32)
    return pl.pallas_call(
        prepare_kernel,
        grid_spec=pltpu.PrefetchScalarGridSpec(
            num_scalar_prefetch=1,
            grid=(channels // wide,),
            in_specs=[column, column],
            out_specs=[out(n) for n in sizes],
            scratch_shapes=[pltpu.VMEM((rows, HEAD_DIM), F32)] * 8,
        ),
        out_shape=[shape(n) for n in sizes],
        name="prepare",
    )(info, keys, values)


def coarse_kernel(q_ref, q1_ref, q2_ref, q3_ref, q4_ref, *scratch):
    work = [
        (slice(j * HEAD_DIM, (j + 1) * HEAD_DIM), fine) for j, fine in enumerate(scratch)
    ]
    for lanes, fine in work:
        fine[...] = q_ref[:, lanes].astype(F32)
    rows = 256
    for out_ref in (q1_ref, q2_ref, q3_ref, q4_ref):
        for lanes, fine in work:
            value = halved(fine, 0, rows)
            out_ref[:, lanes] = value
            fine[0:rows, :] = value.astype(F32)
        rows //= 2


def coarse(queries):
    rows, channels = queries.shape
    wide = 4 * HEAD_DIM
    sizes = (256, 128, 64, 32)
    return pl.pallas_call(
        coarse_kernel,
        grid=(channels // wide,),
        in_specs=[pl.BlockSpec((rows, wide), lambda h: (0, h))],
        out_specs=[pl.BlockSpec((n, wide), lambda h: (0, h)) for n in sizes],
        out_shape=[jax.ShapeDtypeStruct((n, channels), BF16) for n in sizes],
        scratch_shapes=[pltpu.VMEM((rows, HEAD_DIM), F32)] * 4,
        name="coarse",
    )(queries)


def third_kernel(info, x_ref, one_ref, two_ref, o_ref, *scratch):
    odd_core = info[0] == 1
    columns = x_ref.shape[2] // HEAD_DIM
    work = [
        (side, slice(j * HEAD_DIM, (j + 1) * HEAD_DIM), scratch[side * columns + j])
        for side in range(2)
        for j in range(columns)
    ]
    for side, lanes, fine in work:
        fine[...] = x_ref[side, 0:128, lanes].astype(F32)
    for start, out_ref in ((128, one_ref), (192, two_ref)):
        for side, lanes, fine in work:
            derived = halved(fine, 0, 64)
            sent = x_ref[side, start : start + 64, lanes]
            low = jnp.where(odd_core, derived, sent)
            high = jnp.where(odd_core, sent, derived)
            out_ref[side, 0:64, lanes] = low
            out_ref[side, 64:128, lanes] = high
            fine[0:64, :] = low.astype(F32)
            fine[64:128, :] = high.astype(F32)
    for side, lanes, fine in work:
        o_ref[side, :, lanes] = halved(fine, 0, 64)


def third(info, x_halo):
    channels = x_halo.shape[2]
    wide = 4 * HEAD_DIM

    def pair(n):
        return pl.BlockSpec((2, n, wide), lambda h, info: (0, 0, h))

    return pl.pallas_call(
        third_kernel,
        grid_spec=pltpu.PrefetchScalarGridSpec(
            num_scalar_prefetch=1,
            grid=(channels // wide,),
            in_specs=[pair(256)],
            out_specs=[pair(128), pair(128), pair(64)],
            scratch_shapes=[pltpu.VMEM((128, HEAD_DIM), F32)] * 8,
        ),
        out_shape=[jax.ShapeDtypeStruct((2, n, channels), BF16) for n in (128, 128, 64)],
        name="third",
    )(info, x_halo)


def scores_of(queries, keys):
    return lax.dot_general(
        queries, keys, (((1,), (1,)), ((), ())), preferred_element_type=F32
    )


def softmax_stage(jobs):
    scores = []
    for queries, keys, _, bias in jobs:
        score = scores_of(queries, keys)
        scores.append(score if bias is None else score + bias)
    peaks = [jnp.max(score, axis=1, keepdims=True) for score in scores]
    weights = [
        jnp.exp2((score - peak) * LOG2).astype(BF16)
        for score, peak in zip(scores, peaks, strict=True)
    ]
    results = []
    for (_, _, values, _), weight, peak in zip(jobs, weights, peaks, strict=True):
        both = jnp.dot(weight, values, preferred_element_type=F32)
        peak = jnp.broadcast_to(peak, (peak.shape[0], HEAD_DIM))
        results.append((peak, both[:, :HEAD_DIM], both[:, HEAD_DIM:]))
    return results


def stacked(parts):
    return tuple(jnp.concatenate(part, axis=0) for part in zip(*parts, strict=True))


def spread(refs, acc):
    rows = acc[0].shape[0]
    for ref, value in zip(refs, acc, strict=True):
        ref[pl.ds(0, rows, stride=2), :] = value
        ref[pl.ds(1, rows, stride=2), :] = value


def joined(level, refs, rows):
    peak, num, den = level
    coarse_peak, coarse_num, coarse_den = (ref[rows, :] for ref in refs)
    high = jnp.maximum(peak, coarse_peak)
    here = jnp.exp2((peak - high) * LOG2)
    there = 2.0 * jnp.exp2((coarse_peak - high) * LOG2)
    return (high, here * num + there * coarse_num, here * den + there * coarse_den)


def inner_kernel(info, q_ref, k_ref, v_ref, q1, q2, one_ref, s_ref, *rest):
    size = 14
    scratch = rest[-size * HEADS_PER_STEP :]
    n_ref, l_ref = rest[-size * HEADS_PER_STEP - 2 : -size * HEADS_PER_STEP]
    heads = []
    for j in range(HEADS_PER_STEP):
        own = scratch[size * j : size * j + size]
        heads.append((slice(j * HEAD_DIM, (j + 1) * HEAD_DIM), own[:2], own[2:8], own[8:]))

    @pl.when(pl.program_id(0) == 0)
    def _():
        for _, _, windows, _ in heads:
            for ref in windows[1::2]:
                ref[:, HEAD_DIM:] = jnp.ones((ref.shape[0], HEAD_DIM), BF16)

    lanes = slice(0, HEAD_DIM)
    for cols, fines, windows, _ in heads:
        for side, own in enumerate((k_ref, v_ref)):
            z0, z1, z2 = windows[side::2]
            fine = fines[side]
            near = s_ref[side, 0:128, cols]
            sent_one = s_ref[side, 128:192, cols]
            sent_two = s_ref[side, 192:256, cols]
            z0[0:128, lanes] = near
            z0[128:640, lanes] = own[:, cols]
            z0[640:768, lanes] = near
            z1[0:128, lanes] = one_ref[side, 128:256, cols]
            z1[384:512, lanes] = one_ref[side, 0:128, cols]
            fine[0:128, :] = near.astype(F32)
            derived = halved(fine, 0, 64)
            z1[128:192, lanes] = sent_one
            z1[192:256, lanes] = derived
            z1[256:320, lanes] = derived
            z1[320:384, lanes] = sent_one
            fine[128:192, :] = sent_one.astype(F32)
            fine[192:256, :] = derived.astype(F32)
            fine[256:320, :] = sent_one.astype(F32)
            z2[128:192, lanes] = sent_two
            z2[192:256, lanes] = halved(fine, 128, 64)
            z2[0:64, lanes] = halved(fine, 192, 64)
            z2[64:128, lanes] = sent_two

    left, right = bias_of(info, 0), bias_of(info, 1)
    lane = lax.broadcasted_iota(jnp.int32, (1, 192), 1)
    wide = lax.broadcasted_iota(jnp.int32, (1, 384), 1)
    first0 = jnp.where(wide < 128, left, 0.0)
    last0 = jnp.where(wide >= 256, right, 0.0)
    low2 = jnp.where(lane < 128, right, left)
    high2 = jnp.where(lane < 64, right, left)
    first_low = jnp.where(lane < 128, 0.0, left)
    first_high = jnp.where(lane < 64, 0.0, left)
    last_low = jnp.where(lane < 128, right, 0.0)
    last_high = jnp.where(lane < 64, right, 0.0)
    low, high = slice(0, 192), slice(64, 256)
    jobs = []
    for cols, _, (k0, v0, k1, v1, k2, v2), _ in heads:
        jobs += [
            (q2[0:64, cols], k2[low, :], v2[low, :], low2),
            (q2[64:128, cols], k2[high, :], v2[high, :], high2),
            (q1[0:64, cols], k1[0:192, :], v1[0:192, :], first_low),
            (q1[64:128, cols], k1[64:256, :], v1[64:256, :], first_high),
            (q1[128:192, cols], k1[256:448, :], v1[256:448, :], last_low),
            (q1[192:256, cols], k1[320:512, :], v1[320:512, :], last_high),
        ]
        for block in range(4):
            window = slice(block * 128, block * 128 + 384)
            rows = slice(block * 128, block * 128 + 128)
            bias = first0 if block == 0 else last0 if block == 3 else None
            jobs.append((q_ref[rows, cols], k0[window, :], v0[window, :], bias))
    results = softmax_stage(jobs)
    per_head = [results[10 * j : 10 * j + 10] for j in range(HEADS_PER_STEP)]
    for (_, _, _, refs), done in zip(heads, per_head, strict=True):
        spread(refs[0:3], stacked(done[0:2]))
    for (_, _, _, refs), done in zip(heads, per_head, strict=True):
        spread(refs[3:6], joined(stacked(done[2:6]), refs[0:3], slice(None)))
    for (cols, _, _, refs), done in zip(heads, per_head, strict=True):
        for block in range(4):
            rows = slice(block * 128, block * 128 + 128)
            peak, num, den = joined(done[6 + block], refs[3:6], rows)
            n_ref[rows, cols] = num / den
            l_ref[rows, cols] = peak * LOG2 + jnp.log2(den)


def bias_of(info, flag):
    return jnp.where(info[flag] == 1, 0.0, MASKED).astype(F32)


def k_scratch(n):
    return pltpu.VMEM((n, HEAD_DIM), BF16)


def v_scratch(n):
    return pltpu.VMEM((n, 2 * HEAD_DIM), BF16)


def f_scratch(n):
    return pltpu.VMEM((n, HEAD_DIM), F32)


HEADS_PER_STEP = 2


def column_spec(n, start=0):
    return pl.BlockSpec((n, HEADS_PER_STEP * HEAD_DIM), lambda h, info: (0, start + h))


def pair_spec(n, start=0):
    return pl.BlockSpec((2, n, HEADS_PER_STEP * HEAD_DIM), lambda h, info: (0, 0, start + h))


def inner(info, queries, keys, values, coarse_queries, ones, s_halo, part, parts, earlier):
    rows, channels = queries.shape
    steps = channels // (HEADS_PER_STEP * HEAD_DIM) // parts
    start = part * steps
    in_specs = [column_spec(rows, start)] * 3
    in_specs += [column_spec(256, start), column_spec(128, start)]
    in_specs += [pair_spec(256, start), pair_spec(256, start)]
    operands = [info, queries, keys, values, *coarse_queries[:2], ones, s_halo]
    aliases = {}
    if earlier:
        aliases = {len(operands): 0, len(operands) + 1: 1}
        in_specs += [pl.BlockSpec(memory_space=pl.ANY)] * 2
        operands += earlier
    return pl.pallas_call(
        inner_kernel,
        grid_spec=pltpu.PrefetchScalarGridSpec(
            num_scalar_prefetch=1,
            grid=(steps,),
            in_specs=in_specs,
            out_specs=[column_spec(rows, start)] * 2,
            scratch_shapes=(
                [f_scratch(320), f_scratch(320)]
                + [k_scratch(768), v_scratch(768), k_scratch(512), v_scratch(512)]
                + [k_scratch(256), v_scratch(256)]
                + [f_scratch(n) for n in (256, 512) for _ in range(3)]
            )
            * HEADS_PER_STEP,
        ),
        out_shape=[jax.ShapeDtypeStruct((rows, channels), F32)] * 2,
        input_output_aliases=aliases,
        cost_estimate=pl.CostEstimate(
            flops=1_600_000_000 // parts, bytes_accessed=18_000_000 // parts,
            transcendentals=4_000_000 // parts,
        ),
        name="inner",
    )(*operands)


OUTER_SCRATCH = (
    [v_scratch(n) for n in (192, 192)]
    + [v_scratch(n) for n in (128, 128, 128)]
    + [k_scratch(192), k_scratch(192)]
    + [f_scratch(n) for n in (64, 128, 256, 512, 512, 256) for _ in range(3)]
)


def outer_kernel(
    info, q0, q1, q2, q3, q4, x_ref, one_ref, two_ref, a_ref, u_ref, d_ref, g_ref, w_ref, far_ref,
    n_ref, l_ref, o_ref, *scratch,
):
    odd_core = info[0] == 1
    size = len(OUTER_SCRATCH)
    heads = []
    for j in range(HEADS_PER_STEP):
        own = scratch[size * j : size * j + size]
        heads.append((slice(j * HEAD_DIM, (j + 1) * HEAD_DIM), own[:5], own[5:7], own[7:]))

    @pl.when(pl.program_id(0) == 0)
    def _():
        for _, vs, _, refs in heads:
            for ref in vs:
                ref[:, HEAD_DIM:] = jnp.ones((ref.shape[0], HEAD_DIM), BF16)
            for group, base in ((refs[12:15], MASKED), (refs[15:18], MASKED)):
                for ref, value in zip(group, (base, 0.0, 0.0), strict=True):
                    ref[...] = jnp.full(ref.shape, value, F32)

    lanes = slice(0, HEAD_DIM)
    for cols, (v4, v3, v2, v1, v0), (k4, k3), _ in heads:
        for side, (z4, z3) in enumerate(((k4, k3), (v4, v3))):
            z4[0:32, lanes] = u_ref[side, :, cols]
            z4[32:64, lanes] = d_ref[side, :, cols]
            z4[64:96, lanes] = g_ref[side, :, cols]
            z4[96:192, lanes] = w_ref[side, 64:160, cols]
            z3[0:64, lanes] = a_ref[side, :, cols]
            z3[64:128, lanes] = w_ref[side, 0:64, cols]
            z3[128:192, lanes] = far_ref[side, :, cols]
        v2[:, lanes] = two_ref[1, :, cols]
        v1[:, lanes] = one_ref[1, :, cols]
        v0[:, lanes] = x_ref[1, 0:128, cols]
    missing = bias_of(info, 9)
    row = lax.broadcasted_iota(jnp.int32, (128, 128), 0)
    lane = lax.broadcasted_iota(jnp.int32, (128, 128), 1)
    half = row // HALF
    barred = (half != lane // HALF) & (half == info[0])
    quarter = jnp.where(barred, MASKED, missing)
    lane = lax.broadcasted_iota(jnp.int32, (1, 192), 1)
    b4 = lane % 96
    bias4 = jnp.where(
        b4 < 32, bias_of(info, 6), jnp.where(b4 < 64, bias_of(info, 7), bias_of(info, 8))
    )
    bias3 = jnp.where(lane < 64, bias_of(info, 4), bias_of(info, 5))
    jobs = []
    for cols, (v4, v3, v2, v1, v0), (k4, k3), _ in heads:
        jobs += [
            (q4[:, cols], k4[...], v4[...], bias4),
            (q3[:, cols], k3[...], v3[...], bias3),
            (q2[:, cols], two_ref[0, :, cols], v2[...], quarter),
            (q1[:, cols], one_ref[0, :, cols], v1[...], quarter),
            (q0[:, cols], x_ref[0, 0:128, cols], v0[...], missing),
        ]
    results = softmax_stage(jobs)
    per_head = [results[5 * j : 5 * j + 5] for j in range(HEADS_PER_STEP)]
    edge1 = pl.multiple_of(jnp.where(odd_core, 128, 0), 128)
    edge0 = pl.multiple_of(jnp.where(odd_core, 384, 0), 128)
    every = slice(None)
    for (_, _, _, refs), done in zip(heads, per_head, strict=True):
        spread(refs[0:3], done[0])
        for ref, value in zip(refs[12:15], done[4], strict=True):
            ref[pl.ds(edge0, 128), :] = value
        for ref, value in zip(refs[15:18], done[3], strict=True):
            ref[pl.ds(edge1, 128), :] = value
    for (_, _, _, refs), done in zip(heads, per_head, strict=True):
        spread(refs[3:6], joined(done[1], refs[0:3], every))
    for (_, _, _, refs), done in zip(heads, per_head, strict=True):
        spread(refs[6:9], joined(done[2], refs[3:6], every))
    for _, _, _, refs in heads:
        spread(refs[9:12], joined(tuple(ref[...] for ref in refs[15:18]), refs[6:9], every))
    for cols, _, _, refs in heads:
        for block in range(4):
            rows = slice(block * 128, block * 128 + 128)
            level = tuple(ref[rows, :] for ref in refs[12:15])
            peak, num, den = joined(level, refs[9:12], rows)
            peak = peak * LOG2
            inner_log = l_ref[rows, cols]
            high = jnp.maximum(peak, inner_log)
            here = jnp.exp2(peak - high)
            there = jnp.exp2(inner_log - high)
            total = here * num + there * n_ref[rows, cols]
            o_ref[rows, cols] = (total / (here * den + there)).astype(BF16)


def outer(info, queries, coarse_queries, x_halo, one, two, a, u, d, g, swapped, far, nums, logs):
    rows, channels = queries.shape
    width = HEADS_PER_STEP * HEAD_DIM
    return pl.pallas_call(
        outer_kernel,
        grid_spec=pltpu.PrefetchScalarGridSpec(
            num_scalar_prefetch=1,
            grid=(channels // width,),
            in_specs=[
                pl.BlockSpec((128, width), lambda h, info: (3 * info[0], h)),
                pl.BlockSpec((128, width), lambda h, info: (info[0], h)),
                column_spec(128),
                column_spec(64),
                column_spec(32),
            ]
            + [pair_spec(n) for n in (256, 128, 128, 64, 32, 32, 32, 160, 64)]
            + [column_spec(rows), column_spec(rows)],
            out_specs=column_spec(rows),
            scratch_shapes=OUTER_SCRATCH * HEADS_PER_STEP,
        ),
        out_shape=jax.ShapeDtypeStruct((rows, channels), BF16),
        cost_estimate=pl.CostEstimate(
            flops=400_000_000, bytes_accessed=16_000_000, transcendentals=2_000_000
        ),
        name="outer",
    )(
        info, queries, *coarse_queries, x_halo, one, two, a, u, d, g, swapped, far, nums, logs
    )


def project_kernel(a_ref, w_ref, o_ref):
    weight = jnp.concatenate([w_ref[i] for i in range(w_ref.shape[0])], axis=1)
    o_ref[...] = jnp.dot(a_ref[...], weight, preferred_element_type=F32).astype(BF16)


def project(attended, weight):
    rows, channels = attended.shape
    count, _, width = weight.shape
    step = 4
    return pl.pallas_call(
        project_kernel,
        grid=(count // step,),
        in_specs=[
            pl.BlockSpec((rows, channels), lambda j: (0, 0)),
            pl.BlockSpec((step, channels, width), lambda j: (j, 0, 0)),
        ],
        out_specs=pl.BlockSpec((rows, step * width), lambda j: (0, j)),
        out_shape=jax.ShapeDtypeStruct((rows, count * width), BF16),
        name="project",
    )(attended, weight)


def gathered_project_kernel(where, a_ref, w_ref, o_ref):
    half = a_ref.shape[1] // 2
    x = where[0]
    for other_x in range(2):
        total = None
        for y in range(2):
            part = jnp.concatenate([w_ref[y, 0, 0, other_x], w_ref[y, 0, 1, other_x]], axis=1)
            product = jnp.dot(
                a_ref[:, y * half : (y + 1) * half], part, preferred_element_type=F32
            )
            total = product if total is None else total + product
        lane = pl.multiple_of((x if other_x == 0 else 1 - x) * 256, 256)
        o_ref[:, pl.ds(lane, 256)] = total.astype(BF16)


def gathered_project(where, attended, weight):
    rows, channels = attended.shape
    shape = weight.shape
    return pl.pallas_call(
        gathered_project_kernel,
        grid_spec=pltpu.PrefetchScalarGridSpec(
            num_scalar_prefetch=1,
            grid=(shape[1],),
            in_specs=[
                pl.BlockSpec((rows, channels), lambda i, where: (0, 0)),
                pl.BlockSpec((shape[0], 1, *shape[2:]), lambda i, where: (0, i, 0, 0, 0, 0)),
            ],
            out_specs=pl.BlockSpec((rows, channels // shape[1]), lambda i, where: (0, i)),
        ),
        out_shape=jax.ShapeDtypeStruct((rows, channels), BF16),
        cost_estimate=pl.CostEstimate(
            flops=2 * rows * channels * channels, bytes_accessed=12_000_000, transcendentals=0
        ),
        name="project",
    )(where, attended, weight)


PARTS = 1
CTX = ("z", "x", "c")


def permuted(block, target):
    n = lax.axis_size(CTX)
    route = [(d, target(d)) for d in range(n) if 0 <= target(d) < n]
    return lax.ppermute(block, CTX, route)


def layer(queries, keys, values, out_weight):
    n = lax.axis_size(CTX)
    d = lax.axis_index(CTX)
    core, chip_odd = d % 2, (d // 2) % 2
    left3, right3 = d >= 2, d < n - 2
    left4, right4 = d >= 4, d < n - 4
    info = jnp.stack(
        [
            core,
            1 - core,
            core,
            core,
            jnp.where(core == 1, right3, left3).astype(jnp.int32),
            jnp.where(core == 1, left3, right3).astype(jnp.int32),
            left4.astype(jnp.int32),
            right4.astype(jnp.int32),
            jnp.where(chip_odd == 1, left4, right4).astype(jnp.int32),
            jnp.where(core == 1, d < n - 1, d > 0).astype(jnp.int32),
        ]
    )
    channels, width = out_weight.shape
    by_links = width == 128 and lax.axis_size("y") == 2 and lax.axis_size("x") == 2
    if by_links:
        rows = channels // 2
        half = lax.dynamic_slice_in_dim(out_weight, lax.axis_index("y") * rows, rows, 0)
        across = lax.ppermute(half, "x", [(0, 1), (1, 0)])
        weight = lax.all_gather(jnp.stack([half, across]), ("y", "z", "c"), axis=0)
        weight = weight.reshape(2, -1, 2, 2, rows, width)
    else:
        weight = lax.all_gather(out_weight, CTX, axis=1, tiled=True)
        weight = weight.reshape(channels, -1, 128).transpose(1, 0, 2)
    x_send, s_send, ones, l3, l4 = prepare(info, keys, values)
    x_halo = permuted(x_send, lambda i: i + 1 if i % 2 else i - 1)
    s_halo = permuted(s_send, lambda i: i ^ 1)
    a = permuted(l3, lambda i: i - 2 if i % 2 else i + 2)
    up = permuted(l4, lambda i: i + 4)
    down = permuted(l4, lambda i: i - 4)
    diagonal = permuted(l4, lambda i: i - 6 if (i // 2) % 2 else i + 6)
    coarse_queries = coarse(queries)
    state = ()
    for part in range(PARTS):
        state = inner(info, queries, keys, values, coarse_queries, ones, s_halo, part, PARTS, state)
    swapped = permuted(jnp.concatenate([a, up, down, diagonal], axis=1), lambda i: i ^ 1)
    one, two, three = third(info, x_halo)
    far = permuted(three, lambda i: i ^ 1)
    attended = outer(
        info, queries, coarse_queries, x_halo, one, two, a, up, down, diagonal, swapped, far, *state
    )
    if by_links:
        return gathered_project(lax.axis_index("x")[None], attended, weight)
    return project(attended, weight)


def solution(mesh):
    groups, n = mesh.devices.shape
    across = 2 ** ((n // 2).bit_length() // 3)
    grid = Mesh(mesh.devices.reshape(groups, n // (2 * across), across, 2), ("y", *CTX))
    rows = P(("y", *CTX), None)
    return jax.shard_map(
        layer,
        mesh=grid,
        in_specs=(rows, rows, rows, P(None, CTX)),
        out_specs=rows,
        check_vma=False,
    )
```

time: 201 us -> 185 us (0.920)
  starting transfers between devices: 15.9 us -> 70.3 us
  waiting for transfers between devices: 78 us -> 34.8 us
  Pallas kernels: 83.3 us -> 57.8 us
  local copies, waits for them, and re-layouts: 8.25 us -> 3.84 us
  other arithmetic: 0 us -> 2.15 us
    ppermute x7 -> x9, starting transfers between devices: 15.9 us -> 70.3 us  [the longest x8 69.7 us: permuted(): return lax.ppermute(block, CTX, route)]
    ppermute x7 -> x9, waiting for transfers between devices: 77.2 us -> 34.8 us  [the longest x8 27.3 us: permuted(): return lax.ppermute(block, CTX, route)]
    pallas_call x2 -> x4, Pallas kernels: 60.5 us -> 45.3 us  [the longest x1 17 us: inner(): pl.pallas_call(inner_kernel, grid_spec=pltpu.PrefetchScalarGridSpec(num_s...]
    pallas_call x1, Pallas kernels: 10.3 us -> 5.02 us  [third(): pl.pallas_call(third_kernel, grid_spec=pltpu.PrefetchScalarGridSpec(num_s...]
    pallas_call x1, Pallas kernels: 12.4 us -> 7.45 us  [prepare(): pl.pallas_call(prepare_kernel, grid_spec=pltpu.PrefetchScalarGridSpec(num...]
    unnamed x16 -> x14, local copies, waits for them, and re-layouts: 6.88 us -> 3.17 us
  transfers between devices with their start and end apart: 8 -> 10, of which waited for: 3 -> 5; matrix products, arithmetic and copies ran while one was open for 3% -> 1% of each run, Pallas kernels for 37% -> 27%
where the time goes in v2:
time: 185 us; the launch traced here: 182 us
  starting transfers between devices  70.3 us (38%)
  Pallas kernels  57.8 us (31%)
  waiting for transfers between devices  34.8 us (19%)
  between operations  13.5 us (7%)
  local copies, waits for them, and re-layouts  3.84 us (2%)
  other arithmetic  2.15 us (1%)
    ppermute x8, starting transfers between devices, permuted(): return lax.ppermute(block, CTX, route)  69.7 us
    ppermute x8, waiting for transfers between devices, permuted(): return lax.ppermute(block, CTX, route)  27.3 us
    pallas_call x1, Pallas kernels, inner(): pl.pallas_call(inner_kernel, grid_spec=pltpu.PrefetchScalarGridSpec(num_s...  17 us
    pallas_call x1, Pallas kernels, outer(): pl.pallas_call(outer_kernel, grid_spec=pltpu.PrefetchScalarGridSpec(num_s...  15.3 us
    pallas_call x1, Pallas kernels, gathered_project(): pl.pallas_call(gathered_project_kernel, grid_spec=pltpu.PrefetchScalarGri...  8.79 us
    ppermute x1, waiting for transfers between devices, layer(): across = lax.ppermute(half, 'x', [(0, 1), (1, 0)])  7.49 us
    pallas_call x1, Pallas kernels, prepare(): pl.pallas_call(prepare_kernel, grid_spec=pltpu.PrefetchScalarGridSpec(num...  7.45 us
    pallas_call x1, Pallas kernels, third(): pl.pallas_call(third_kernel, grid_spec=pltpu.PrefetchScalarGridSpec(num_s...  5.02 us
  transfers between devices with their start and end apart: 10, of which 5 were waited for; matrix products, arithmetic and copies ran while one was open for 1% of the time, Pallas kernels for 27%

profile of v2, /device:TPU:10, one launch (start us, length us, event | category | flops | bytes accessed | tf_op | source)
XLA Modules:
  0.0 182.5 jit_solution(6562582736891964026)
XLA Ops:
  6.5 1.0 copy-done
  8.2 7.5 %collective-permute-done.8 = bf16[1024,128]{1,0:T(8,128)(2,1)S(1)} collective-permute-done((bf16[1024,128]{1,0:T(8,128)(2,1)S(1)}, bf16[1024,128]{1,0:T(8,128)(2,1)S(1)}, u32[]{:S(2)}, u32[]{:S(2)}) %collective-permute-start.8) | collective-permute-done | bytes 262176 | tf_op jit(solution)/shard_map/ppermute | solution.py:582
  15.7 0.9 pad_maximum_fusion.1
  16.7 0.6 stack.70.info
  17.3 7.4 %prepare.1 = (bf16[2,256,2048]{2,1,0:T(8,128)(2,1)}, bf16[2,256,2048]{2,1,0:T(8,128)(2,1)}, bf16[2,256,2048]{2,1,0:T(8,128)(2,1)}, bf16[2,64,2048]{2,1,0:T(8,128)(2,1)}, bf16[2,32,2048]{2,1,0:T(8,128)(2,1)}) custom-call(s32[10]{0:T(128)} %stack.70.info, bf16[512,2048]{1,0:T(8,128)(2,1)} %k_ref.3, bf16[512,2048]{1,0:T(8,128)(2,1)} %v_ref.3), custom_call_target="tpu_custom_call" | custom-call | tf_op jit(solution)/shard_map/prepare/pallas_call | solution.py:84
  24.8 1.9 %collective-permute-start = (bf16[2,256,2048]{2,1,0:T(8,128)(2,1)}, bf16[2,256,2048]{2,1,0:T(8,128)(2,1)S(1)}, u32[]{:S(2)}, u32[]{:S(2)}) collective-permute-start(bf16[2,256,2048]{2,1,0:T(8,128)(2,1)} %get-tuple-element.23), channel_id=1, source_target_pairs={{1,2},{2,1},{3,4},{4,3},{5,6},{6,5},{7,8},{8,7},{9,10},{10,9},{11,... | collective-permute-start | bytes 6291464 | tf_op jit(solution)/shard_map/ppermute | solution.py:554
  26.7 1.7 collective-permute-start.7
  28.4 3.5 %collective-permute-start.2 = (bf16[2,32,2048]{2,1,0:T(8,128)(2,1)}, bf16[2,32,2048]{2,1,0:T(8,128)(2,1)S(1)}, u32[]{:S(2)}, u32[]{:S(2)}) collective-permute-start(bf16[2,32,2048]{2,1,0:T(8,128)(2,1)} %get-tuple-element.27), channel_id=1, source_target_pairs={{0,4},{1,5},{2,6},{3,7},{4,8},{5,9},{6,10},{7,11},{8,12},{9,13},{1... | collective-permute-start | bytes 786440 | tf_op jit(solution)/shard_map/ppermute | solution.py:554
  31.9 3.4 %collective-permute-start.1 = (bf16[2,64,2048]{2,1,0:T(8,128)(2,1)}, bf16[2,64,2048]{2,1,0:T(8,128)(2,1)S(1)}, u32[]{:S(2)}, u32[]{:S(2)}) collective-permute-start(bf16[2,64,2048]{2,1,0:T(8,128)(2,1)} %get-tuple-element.26), channel_id=1, source_target_pairs={{0,2},{2,4},{3,1},{4,6},{5,3},{6,8},{7,5},{8,10},{9,7},{10,12},{11... | collective-permute-start | bytes 1572872 | tf_op jit(solution)/shard_map/ppermute | solution.py:554
  35.3 2.4 %collective-permute-start.3 = (bf16[2,32,2048]{2,1,0:T(8,128)(2,1)}, bf16[2,32,2048]{2,1,0:T(8,128)(2,1)S(1)}, u32[]{:S(2)}, u32[]{:S(2)}) collective-permute-start(bf16[2,32,2048]{2,1,0:T(8,128)(2,1)} %get-tuple-element.27), channel_id=1, source_target_pairs={{4,0},{5,1},{6,2},{7,3},{8,4},{9,5},{10,6},{11,7},{12,8},{13,9},{1... | collective-permute-start | bytes 786440 | tf_op jit(solution)/shard_map/ppermute | solution.py:554
  37.6 9.0 %collective-permute-done.2.u_ref = bf16[2,32,2048]{2,1,0:T(8,128)(2,1)S(1)} collective-permute-done((bf16[2,32,2048]{2,1,0:T(8,128)(2,1)}, bf16[2,32,2048]{2,1,0:T(8,128)(2,1)S(1)}, u32[]{:S(2)}, u32[]{:S(2)}) %collective-permute-start.2) | collective-permute-done | bytes 262176 | tf_op jit(solution)/shard_map/ppermute | solution.py:554
  46.7 1.9 %collective-permute-start.4 = (bf16[2,32,2048]{2,1,0:T(8,128)(2,1)}, bf16[2,32,2048]{2,1,0:T(8,128)(2,1)S(1)}, u32[]{:S(2)}, u32[]{:S(2)}) collective-permute-start(bf16[2,32,2048]{2,1,0:T(8,128)(2,1)} %get-tuple-element.27), channel_id=1, source_target_pairs={{0,6},{1,7},{4,10},{5,11},{6,0},{7,1},{8,14},{9,15},{10,4},{11,5},... | collective-permute-start | bytes 786440 | tf_op jit(solution)/shard_map/ppermute | solution.py:554
  48.6 2.5 %collective-permute-done.3.d_ref = bf16[2,32,2048]{2,1,0:T(8,128)(2,1)S(1)} collective-permute-done((bf16[2,32,2048]{2,1,0:T(8,128)(2,1)}, bf16[2,32,2048]{2,1,0:T(8,128)(2,1)S(1)}, u32[]{:S(2)}, u32[]{:S(2)}) %collective-permute-start.3) | collective-permute-done | bytes 262176 | tf_op jit(solution)/shard_map/ppermute | solution.py:554
  51.1 7.4 %collective-permute-done.4.g_ref = bf16[2,32,2048]{2,1,0:T(8,128)(2,1)S(1)} collective-permute-done((bf16[2,32,2048]{2,1,0:T(8,128)(2,1)}, bf16[2,32,2048]{2,1,0:T(8,128)(2,1)S(1)}, u32[]{:S(2)}, u32[]{:S(2)}) %collective-permute-start.4) | collective-permute-done | bytes 262176 | tf_op jit(solution)/shard_map/ppermute | solution.py:554
  58.5 8.4 %collective-permute-done.1.a_ref = bf16[2,64,2048]{2,1,0:T(8,128)(2,1)S(1)} collective-permute-done((bf16[2,64,2048]{2,1,0:T(8,128)(2,1)}, bf16[2,64,2048]{2,1,0:T(8,128)(2,1)S(1)}, u32[]{:S(2)}, u32[]{:S(2)}) %collective-permute-start.1) | collective-permute-done | bytes 524320 | tf_op jit(solution)/shard_map/ppermute | solution.py:554
  66.9 1.3 pad_maximum_fusion
  68.1 54.9 %collective-permute-start.5 = (bf16[2,160,2048]{2,1,0:T(8,128)(2,1)}, bf16[2,160,2048]{2,1,0:T(8,128)(2,1)}, u32[]{:S(2)}, u32[]{:S(2)}) collective-permute-start(bf16[2,160,2048]{2,1,0:T(8,128)(2,1)} %pad_maximum_fusion), channel_id=1, source_target_pairs={{0,1},{1,0},{2,3},{3,2},{4,5},{5,4},{6,7},{7,6},{8,9},{9,8},{10,11... | collective-permute-start | bytes 3932168 | tf_op jit(solution)/shard_map/ppermute | solution.py:554
  123.0 1.3 copy-done.1
  124.4 5.0 %third.1 = (bf16[2,128,2048]{2,1,0:T(8,128)(2,1)}, bf16[2,128,2048]{2,1,0:T(8,128)(2,1)}, bf16[2,64,2048]{2,1,0:T(8,128)(2,1)}) custom-call(s32[10]{0:T(128)} %stack.70.info, bf16[2,256,2048]{2,1,0:T(8,128)(2,1)} %copy-done.1), custom_call_target="tpu_custom_call" | custom-call | tf_op jit(solution)/shard_map/third/pallas_call | solution.py:159
  129.5 4.2 %coarse.1 = (bf16[256,2048]{1,0:T(8,128)(2,1)}, bf16[128,2048]{1,0:T(8,128)(2,1)}, bf16[64,2048]{1,0:T(8,128)(2,1)}, bf16[32,2048]{1,0:T(8,128)(2,1)}) custom-call(bf16[512,2048]{1,0:T(8,128)(2,1)} %q0.1), custom_call_target="tpu_custom_call" | custom-call | tf_op jit(solution)/shard_map/coarse/pallas_call | solution.py:117
  133.6 17.0 %inner.1 = (f32[512,2048]{1,0:T(8,128)}, f32[512,2048]{1,0:T(8,128)}) custom-call(s32[10]{0:T(128)} %stack.70.info, bf16[512,2048]{1,0:T(8,128)(2,1)} %q0.1, bf16[512,2048]{1,0:T(8,128)(2,1)} %k_ref.3, bf16[512,2048]{1,0:T(8,128)(2,1)} %v_ref.3, bf16[256,2048]{1,0:T(8,128)(2,1)} %get-tuple-element.19.q1, bf16[128,2048]{1,0:T(8,128)(2,1)} %get-tuple-element.20.q2, ...), custom_call_target="tpu_custom_call" | custom-call | flops 1600000000 | bytes 18000000 | tf_op jit(solution)/shard_map/inner/pallas_call | solution.py:340
  150.7 0.8 copy-done.6
  151.5 15.3 %outer.1.a_ref = bf16[512,2048]{1,0:T(8,128)(2,1)} custom-call(s32[10]{0:T(128)} %stack.70.info, bf16[512,2048]{1,0:T(8,128)(2,1)} %q0.1, bf16[256,2048]{1,0:T(8,128)(2,1)} %get-tuple-element.19.q1, bf16[128,2048]{1,0:T(8,128)(2,1)} %get-tuple-element.20.q2, bf16[64,2048]{1,0:T(8,128)(2,1)} %get-tuple-element.21.q3, bf16[32,2048]{1,0:T(8,128)(2,1)} %get-tuple-element.22.q4, ...), custom_call_target="tpu_custom_call" | custom-call | flops 400000000 | bytes 16000000 | tf_op jit(solution)/shard_map/outer/pallas_call | solution.py:461
  166.9 8.8 %project.1 = bf16[512,2048]{1,0:T(8,128)(2,1)} custom-call(s32[1]{0:T(128)} %bitcast.where, bf16[512,2048]{1,0:T(8,128)(2,1)} %outer.1.a_ref, bf16[2,4,2,2,1024,128]{5,4,3,2,1,0:T(8,128)(2,1)} %bitcast.14), custom_call_target="tpu_custom_call" | custom-call | flops 4294967296 | bytes 12000000 | tf_op jit(solution)/shard_map/project/pallas_call | solution.py:528
  (22 shorter events, 0.8 us)
Async XLA Ops:
  6.5 1.0 copy-start
  6.5 160.3 %all-gather.3.cloned.1.call-start = ((), (), s32[]{:S(2)}) async-start(), calls=%async_computation | async-start | bytes 8912896 | tf_op jit(solution)/shard_map/all_gather | solution.py:583
  7.6 8.1 %collective-permute-start.8 = (bf16[1024,128]{1,0:T(8,128)(2,1)S(1)}, bf16[1024,128]{1,0:T(8,128)(2,1)S(1)}, u32[]{:S(2)}, u32[]{:S(2)}) collective-permute-start(bf16[1024,128]{1,0:T(8,128)(2,1)S(1)} %constant_dynamic-slice_fusion), channel_id=1, source_target_pairs={{0,2},{2,0},{1,3},{3,1},{4,6},{6,4},{5,7},{7,5},{8,10},{10,8},{9,1... | collective-permute-start | bytes 786440 | tf_op jit(solution)/shard_map/ppermute | solution.py:582
  24.8 98.3 %collective-permute-start = (bf16[2,256,2048]{2,1,0:T(8,128)(2,1)}, bf16[2,256,2048]{2,1,0:T(8,128)(2,1)S(1)}, u32[]{:S(2)}, u32[]{:S(2)}) collective-permute-start(bf16[2,256,2048]{2,1,0:T(8,128)(2,1)} %get-tuple-element.23), channel_id=1, source_target_pairs={{1,2},{2,1},{3,4},{4,3},{5,6},{6,5},{7,8},{8,7},{9,10},{10,9},{11,... | collective-permute-start | bytes 6291464 | tf_op jit(solution)/shard_map/ppermute | solution.py:554
  26.7 107.0 %collective-permute-start.7 = (bf16[2,256,2048]{2,1,0:T(8,128)(2,1)}, bf16[2,256,2048]{2,1,0:T(8,128)(2,1)}, u32[]{:S(2)}, u32[]{:S(2)}) collective-permute-start(bf16[2,256,2048]{2,1,0:T(8,128)(2,1)} %get-tuple-element.30), channel_id=1, source_target_pairs={{0,1},{1,0},{2,3},{3,2},{4,5},{5,4},{6,7},{7,6},{8,9},{9,8},{10,11... | collective-permute-start | bytes 6291464 | tf_op jit(solution)/shard_map/ppermute | solution.py:554
  28.4 18.3 %collective-permute-start.2 = (bf16[2,32,2048]{2,1,0:T(8,128)(2,1)}, bf16[2,32,2048]{2,1,0:T(8,128)(2,1)S(1)}, u32[]{:S(2)}, u32[]{:S(2)}) collective-permute-start(bf16[2,32,2048]{2,1,0:T(8,128)(2,1)} %get-tuple-element.27), channel_id=1, source_target_pairs={{0,4},{1,5},{2,6},{3,7},{4,8},{5,9},{6,10},{7,11},{8,12},{9,13},{1... | collective-permute-start | bytes 786440 | tf_op jit(solution)/shard_map/ppermute | solution.py:554
  31.9 35.0 %collective-permute-start.1 = (bf16[2,64,2048]{2,1,0:T(8,128)(2,1)}, bf16[2,64,2048]{2,1,0:T(8,128)(2,1)S(1)}, u32[]{:S(2)}, u32[]{:S(2)}) collective-permute-start(bf16[2,64,2048]{2,1,0:T(8,128)(2,1)} %get-tuple-element.26), channel_id=1, source_target_pairs={{0,2},{2,4},{3,1},{4,6},{5,3},{6,8},{7,5},{8,10},{9,7},{10,12},{11... | collective-permute-start | bytes 1572872 | tf_op jit(solution)/shard_map/ppermute | solution.py:554
  35.3 15.8 %collective-permute-start.3 = (bf16[2,32,2048]{2,1,0:T(8,128)(2,1)}, bf16[2,32,2048]{2,1,0:T(8,128)(2,1)S(1)}, u32[]{:S(2)}, u32[]{:S(2)}) collective-permute-start(bf16[2,32,2048]{2,1,0:T(8,128)(2,1)} %get-tuple-element.27), channel_id=1, source_target_pairs={{4,0},{5,1},{6,2},{7,3},{8,4},{9,5},{10,6},{11,7},{12,8},{13,9},{1... | collective-permute-start | bytes 786440 | tf_op jit(solution)/shard_map/ppermute | solution.py:554
  46.7 82.7 %copy-start.3 = (bf16[2,32,2048]{2,1,0:T(8,128)(2,1)}, bf16[2,32,2048]{2,1,0:T(8,128)(2,1)S(1)}, u32[]{:S(2)}) copy-start(bf16[2,32,2048]{2,1,0:T(8,128)(2,1)S(1)} %collective-permute-done.2.u_ref) | copy-start | bytes 786436
  46.7 11.8 %collective-permute-start.4 = (bf16[2,32,2048]{2,1,0:T(8,128)(2,1)}, bf16[2,32,2048]{2,1,0:T(8,128)(2,1)S(1)}, u32[]{:S(2)}, u32[]{:S(2)}) collective-permute-start(bf16[2,32,2048]{2,1,0:T(8,128)(2,1)} %get-tuple-element.27), channel_id=1, source_target_pairs={{0,6},{1,7},{4,10},{5,11},{6,0},{7,1},{8,14},{9,15},{10,4},{11,5},... | collective-permute-start | bytes 786440 | tf_op jit(solution)/shard_map/ppermute | solution.py:554
  51.1 17.0 %copy-start.4 = (bf16[2,32,2048]{2,1,0:T(8,128)(2,1)}, bf16[2,32,2048]{2,1,0:T(8,128)(2,1)S(1)}, u32[]{:S(2)}) copy-start(bf16[2,32,2048]{2,1,0:T(8,128)(2,1)S(1)} %collective-permute-done.3.d_ref) | copy-start | bytes 786436
  58.5 64.5 %copy-start.5 = (bf16[2,32,2048]{2,1,0:T(8,128)(2,1)}, bf16[2,32,2048]{2,1,0:T(8,128)(2,1)S(1)}, u32[]{:S(2)}) copy-start(bf16[2,32,2048]{2,1,0:T(8,128)(2,1)S(1)} %collective-permute-done.4.g_ref) | copy-start | bytes 786436
  66.9 62.5 %copy-start.2 = (bf16[2,64,2048]{2,1,0:T(8,128)(2,1)}, bf16[2,64,2048]{2,1,0:T(8,128)(2,1)S(1)}, u32[]{:S(2)}) copy-start(bf16[2,64,2048]{2,1,0:T(8,128)(2,1)S(1)} %collective-permute-done.1.a_ref) | copy-start | bytes 1572868
  68.1 82.5 %collective-permute-start.5 = (bf16[2,160,2048]{2,1,0:T(8,128)(2,1)}, bf16[2,160,2048]{2,1,0:T(8,128)(2,1)}, u32[]{:S(2)}, u32[]{:S(2)}) collective-permute-start(bf16[2,160,2048]{2,1,0:T(8,128)(2,1)} %pad_maximum_fusion), channel_id=1, source_target_pairs={{0,1},{1,0},{2,3},{3,2},{4,5},{5,4},{6,7},{7,6},{8,9},{9,8},{10,11... | collective-permute-start | bytes 3932168 | tf_op jit(solution)/shard_map/ppermute | solution.py:554
  123.0 1.3 copy-start.1
  129.4 21.3 %collective-permute-start.6 = (bf16[2,64,2048]{2,1,0:T(8,128)(2,1)}, bf16[2,64,2048]{2,1,0:T(8,128)(2,1)S(1)}, u32[]{:S(2)}, u32[]{:S(2)}) collective-permute-start(bf16[2,64,2048]{2,1,0:T(8,128)(2,1)} %get-tuple-element.28), channel_id=1, source_target_pairs={{0,1},{1,0},{2,3},{3,2},{4,5},{5,4},{6,7},{7,6},{8,9},{9,8},{10,11... | collective-permute-start | bytes 1572872 | tf_op jit(solution)/shard_map/ppermute | solution.py:554
  150.7 0.8 copy-start.6
Sparse Core Ops, SparseCore 0:
  16.7 97.7 all-gather.2
